TPU v7x, 768 devices: a whole 4x8x12 slice. The times are simulated.
768 devices in a mesh: scene: 96 (over z, x, core), seq: 8 (over y).
Axes of the slice: x: 4, y: 8, z: 12, core: 2. Of those that a mesh axis runs over, the one named last changes fastest.
Arguments:
- qkv: bfloat16 [3, 98304, 1280], P(None, ('scene', 'seq')), may hold values from -6.5 to 6.5
- view_counts: int32 [96], P('scene'), may hold values from 1 to 2, as said below
- out_weight: bfloat16 [1280, 1280], replicated, may hold values from -0.15625 to 0.15625
- out_cotangent: bfloat16 [98304, 1280], P(('scene', 'seq')), may hold values from -6 to 6
Outputs:
- d_qkv: bfloat16 [3, 98304, 1280], P(None, ('scene', 'seq'))
- weight_grad: float32 [1280, 1280], P('seq')
Inputs may be any that keep to these rules, and one draw needn't show every extreme that they name: `view_counts`: some scene has 2 views and some 1.
All inputs are finite; a program needn't handle non-finite values.
Results may differ from a plain program's by a relative error of at most 0.0065.
Values may be sent and summed in bfloat16 or wider, within the bound.
A program may use at most 64 MiB of HBM per device.

v0:
```python
import math

import jax
import jax.numpy as jnp
from jax import lax
from jax.sharding import PartitionSpec as P

HD = 64
HV = 12
TV = 512
VMAX = 2


def attend(queries, keys, values, key_live, query_live):
    scale = 1.0 / math.sqrt(queries.shape[-1])
    scores = (
        jnp.einsum("blhd,bmhd->bhlm", queries, keys, preferred_element_type=jnp.float32) * scale
    )
    scores = jnp.where(key_live[:, None, None, :] > 0.5, scores, -1e30)
    probs = jax.nn.softmax(scores, axis=-1)
    rounded = probs.astype(jnp.bfloat16)
    outputs = jnp.einsum("bhlm,bmhd->blhd", rounded, values, preferred_element_type=jnp.float32)
    return (outputs * query_live[:, :, None, None], probs, rounded)


def attend_back(queries, keys, values, probs, rounded, query_live, grad_out):
    scale = 1.0 / math.sqrt(queries.shape[-1])
    grad_in = grad_out * query_live[:, :, None, None].astype(jnp.bfloat16)
    grad_values = jnp.einsum(
        "bhlm,blhd->bmhd", rounded, grad_in, preferred_element_type=jnp.float32
    )
    grad_probs = jnp.einsum("blhd,bmhd->bhlm", grad_in, values, preferred_element_type=jnp.float32)
    grad_scores = probs * (grad_probs - jnp.sum(probs * grad_probs, axis=-1, keepdims=True)) * scale
    grad_queries = jnp.einsum("bhlm,bmhd->blhd", grad_scores, keys.astype(jnp.float32))
    grad_keys = jnp.einsum("bhlm,blhd->bmhd", grad_scores, queries.astype(jnp.float32))
    return jnp.stack([grad_queries, grad_keys, grad_values]).astype(jnp.bfloat16)


def on_device(qkv, view_counts, out_weight, out_cotangent):
    width = qkv.shape[2]
    tok_rows = qkv.shape[1]
    seq_parts = lax.axis_size("seq")
    seq_index = lax.axis_index("seq")
    places = tok_rows // VMAX
    groups = seq_parts // VMAX
    view_width = HV * HD
    group_width = view_width // groups
    group_heads = HV // groups
    cross_width = width - view_width
    cross_heads = cross_width // HD
    view_count = view_counts[0]
    live_all = (jnp.arange(VMAX) < view_count).astype(jnp.float32)
    local = qkv.reshape(3, places, VMAX, width)
    view_part = local[..., :view_width].reshape(3, places, VMAX * groups, group_width)
    contract_last = (((1,), (1,)), ((), ()))
    grad_all = lax.dot_general(
        out_cotangent, out_weight, contract_last, preferred_element_type=jnp.float32
    ).astype(jnp.bfloat16)
    grad_view = grad_all[:, :view_width].reshape(1, places, VMAX * groups, group_width)
    arrived, grad_arrived = (
        lax.all_to_all(view_part, "seq", split_axis=2, concat_axis=1, tiled=True),
        lax.all_to_all(grad_view, "seq", split_axis=2, concat_axis=1, tiled=True),
    )
    my_view = seq_index // groups
    view_live = (my_view < view_count).astype(jnp.float32)
    query_live = jnp.broadcast_to(view_live, (1, TV))
    all_keys = jnp.ones((1, TV), jnp.float32)
    heads_in = arrived.reshape(3, TV, group_heads, HD).transpose(2, 0, 1, 3)
    grad_heads = grad_arrived.reshape(TV, group_heads, HD).transpose(1, 0, 2)

    def one_head(item):
        stacked, grad_one = item
        queries = stacked[0][None, :, None, :]
        keys = stacked[1][None, :, None, :]
        values = stacked[2][None, :, None, :]
        out_one, probs, rounded = attend(queries, keys, values, all_keys, query_live)
        grads = attend_back(
            queries, keys, values, probs, rounded, query_live, grad_one[None, :, None, :]
        )
        return (out_one.astype(jnp.bfloat16)[0, :, 0, :], grads[:, 0, :, 0, :])

    head_outs, head_grads = lax.map(one_head, (heads_in, grad_heads))
    view_out = head_outs.transpose(1, 0, 2).reshape(1, TV, 1, group_width)
    view_grads = head_grads.transpose(1, 2, 0, 3).reshape(3, TV, 1, group_width)
    grads_home, out_home = (
        lax.all_to_all(view_grads, "seq", split_axis=1, concat_axis=2, tiled=True),
        lax.all_to_all(view_out, "seq", split_axis=1, concat_axis=2, tiled=True),
    )
    grads_home = grads_home.reshape(3, places, VMAX, view_width)
    out_home = out_home.reshape(places, VMAX, view_width)
    cross = local[..., view_width:].reshape(3, places, VMAX, cross_heads, HD)
    cross_keep = jnp.broadcast_to(live_all[None, :], (places, VMAX))
    cross_out, cross_probs, cross_rounded = attend(
        cross[0], cross[1], cross[2], cross_keep, cross_keep
    )
    cross_grad_in = grad_all[:, view_width:].reshape(places, VMAX, cross_heads, HD)
    cross_grads = attend_back(
        cross[0], cross[1], cross[2], cross_probs, cross_rounded, cross_keep, cross_grad_in
    ).reshape(3, places, VMAX, cross_width)
    cross_flat = cross_out.astype(jnp.bfloat16).reshape(places, VMAX, cross_width)
    attn_flat = jnp.concatenate([out_home, cross_flat], axis=-1).reshape(tok_rows, width)
    d_qkv = jnp.concatenate([grads_home, cross_grads], axis=-1).reshape(3, tok_rows, width)
    feature_cols = lax.all_to_all(attn_flat, "seq", split_axis=1, concat_axis=0, tiled=True)
    contract_first = (((0,), (0,)), ((), ()))
    grad_rows = lax.dot_general(
        feature_cols,
        lax.all_gather(out_cotangent, "seq", axis=0, tiled=True),
        contract_first,
        preferred_element_type=jnp.float32,
    )
    grad_rows = lax.psum(grad_rows, "scene")
    weight_grad = grad_rows * (1.0 / math.sqrt(lax.axis_size("scene") * seq_parts * tok_rows))
    return (d_qkv, weight_grad)


def solution(mesh):
    in_specs = (P(None, ("scene", "seq"), None), P("scene"), P(), P(("scene", "seq"), None))
    out_specs = (P(None, ("scene", "seq"), None), P("seq", None))
    return jax.shard_map(
        on_device, mesh=mesh, in_specs=in_specs, out_specs=out_specs, check_vma=False
    )
```

profile of v0, /device:TPU:1, one launch (start us, length us, event | category | flops | bytes accessed | tf_op | source)
XLA Modules:
  0.0 447.5 jit_solution(5321927236768488184)
XLA Ops:
  7.2 1.9 copy-done
  9.1 2.2 convolution_convert_fusion.3
  14.6 7.6 %all-to-all-start.1 = ((bf16[1,64,8,192]{3,1,0,2:T(8,128)(2,1)}), bf16[1,64,8,192]{3,1,0,2:T(8,128)(2,1)}, u32[]{:S(2)}, u32[]{:S(2)}) async-start(bf16[1,64,8,192]{3,1,0,2:T(8,128)(2,1)} %copy.63), calls=%async_computation.1 | async-start | bytes 524288 | tf_op jit(solution)/shard_map/all_to_all | solution.py:62
  22.3 3.2 reshape.277
  25.4 2.3 slice.52
  27.7 3.0 reshape.278
  30.7 2.2 copy.61
  32.9 6.6 %all-to-all-start = ((bf16[3,64,8,192]{3,1,0,2:T(8,128)(2,1)}), bf16[3,64,8,192]{3,1,0,2:T(8,128)(2,1)}, u32[]{:S(2)}, u32[]{:S(2)}) async-start(bf16[3,64,8,192]{3,1,0,2:T(8,128)(2,1)} %copy.61), calls=%async_computation | async-start | bytes 1572864 | tf_op jit(solution)/shard_map/all_to_all | solution.py:61
  41.0 2.0 fusion.57
  43.0 1.9 reshape.289
  44.8 1.9 reshape.288
  48.5 4.3 fusion.58
  52.8 1.9 copy.64
  56.0 2.5 copy.62
  58.5 2.7 reshape.279
  61.2 28.9 %while.14 = (s32[]{:T(128)}, bf16[3,512,64]{1,2,0:T(8,128)(2,1)}, bf16[3,3,512,64]{2,3,0,1:T(8,128)(2,1)}, bf16[3,3,512,64]{2,3,0,1:T(8,128)(2,1)}, bf16[3,512,6...) while((s32[]{:T(128)}, bf16[3,512,64]{1,2,0:T(8,128)(2,1)}, ...), condition=%wide.region_4.5_spmd.clone, body=%wide.region_0.4_spmd.clone.sunk | while | flops 208435712 | bytes 21926172 | solution.py:82
  61.2 1.3 fusion.80
  62.7 1.8 fusion.82
  64.7 1.6 fusion.83
  70.8 1.3 fusion.80
  72.3 1.9 fusion.82
  74.3 1.6 fusion.83
  80.4 1.3 fusion.80
  81.9 1.9 fusion.82
  83.9 1.6 fusion.83
  90.0 1.9 copy.84
  92.5 3.2 reduce.9
  96.6 6.6 %all-to-all-start.3 = ((bf16[8,2,6144]{2,1,0:T(2,128)(2,1)}), bf16[8,2,6144]{2,1,0:T(2,128)(2,1)}, u32[]{:S(2)}, u32[]{:S(2)}) async-start(bf16[8,2,6144]{2,1,0:T(2,128)(2,1)} %reshape.291), calls=%async_computation.3 | async-start | bytes 393216 | tf_op jit(solution)/shard_map/all_to_all | solution.py:87
  103.3 4.1 multiply_reduce_fusion.1
  109.1 2.9 all-to-all-done.3
  112.0 2.0 reshape.292
  116.2 1.8 pad_maximum_fusion
  117.9 1.9 copy.89
  119.8 4.1 all-to-all-start.4
  123.9 2.3 copy.68
  126.3 7.7 %all-to-all-done.4 = bf16[128,8,160]{0,2,1:T(8,128)(2,1)} async-done(((bf16[128,8,160]{0,2,1:T(8,128)(2,1)}), bf16[128,8,160]{0,2,1:T(8,128)(2,1)}, u32[]{:S(2)}, u32[]{:S(2)}) %all-to-all-start.4) | async-done | bytes 327712 | tf_op jit(solution)/shard_map/all_to_all | solution.py:103
  134.0 4.2 all-to-all-start.2
  138.3 1.8 fusion.42
  141.0 2.0 fusion.41
  143.9 3.4 fusion.43
  147.4 2.1 fusion.40
  150.3 5.1 %all-to-all-done.2 = bf16[3,512,1,192]{3,0,2,1:T(4,128)(2,1)} async-done(((bf16[3,512,1,192]{3,0,2,1:T(4,128)(2,1)}), bf16[3,512,1,192]{3,0,2,1:T(4,128)(2,1)}, u32[]{:S(2)}, u32[]{:S(2)}) %all-to-all-start.2) | async-done | bytes 589856 | tf_op jit(solution)/shard_map/all_to_all | solution.py:86
  155.4 1.3 copy.69
  156.7 1.3 copy.70
  158.1 2.6 concatenate.28
  160.6 2.1 maximum_maximum_fusion
  162.8 275.7 %all-reduce.2.cloned.1.call-done = f32[160,1280]{1,0:T(8,128)} async-done(((f32[160,1280]{1,0:T(8,128)}), f32[160,1280]{1,0:T(8,128)}) %all-reduce.2.cloned.1.call-update) | async-done | bytes 819216 | tf_op jit(solution)/shard_map/psum | solution.py:111
  438.5 2.1 broadcast_multiply_fusion
  (93 shorter events, 29.8 us)
Async XLA Ops:
  7.2 1.9 copy-start
  11.3 0.7 copy-start.5
  14.6 18.3 %all-to-all-start.1 = ((bf16[1,64,8,192]{3,1,0,2:T(8,128)(2,1)}), bf16[1,64,8,192]{3,1,0,2:T(8,128)(2,1)}, u32[]{:S(2)}, u32[]{:S(2)}) async-start(bf16[1,64,8,192]{3,1,0,2:T(8,128)(2,1)} %copy.63), calls=%async_computation.1 | async-start | bytes 524288 | tf_op jit(solution)/shard_map/all_to_all | solution.py:62
  30.7 16.9 %slice-start = ((bf16[128,1280]{1,0:T(8,128)(2,1)}), bf16[128,512]{1,0:T(8,128)(2,1)S(1)}, s32[]{:S(2)}) async-start(bf16[128,1280]{1,0:T(8,128)(2,1)} %copy-done.5), calls=%async_computation.7 | async-start | bytes 262144 | tf_op jit(solution)/shard_map/slice | solution.py:96
  32.9 23.1 %all-to-all-start = ((bf16[3,64,8,192]{3,1,0,2:T(8,128)(2,1)}), bf16[3,64,8,192]{3,1,0,2:T(8,128)(2,1)}, u32[]{:S(2)}, u32[]{:S(2)}) async-start(bf16[3,64,8,192]{3,1,0,2:T(8,128)(2,1)} %copy.61), calls=%async_computation | async-start | bytes 1572864 | tf_op jit(solution)/shard_map/all_to_all | solution.py:61
  39.6 104.4 %all-gather.2.cloned.1.call-start = ((), (), s32[]{:S(2)}) async-start(), calls=%async_computation.5 | async-start | bytes 2949120 | tf_op jit(solution)/shard_map/all_gather | solution.py:107
  61.2 3.4 copy-start.3
  62.5 2.1 copy-start.1
  64.7 1.6 copy-start.2
  68.8 2.0 copy-start.4
  70.8 3.4 copy-start.3
  72.1 2.1 copy-start.1
  74.3 1.6 copy-start.2
  78.4 2.0 copy-start.4
  80.4 3.4 copy-start.3
  81.7 2.1 copy-start.1
  83.9 1.7 copy-start.2
  88.0 2.0 copy-start.4
  96.6 15.3 %all-to-all-start.3 = ((bf16[8,2,6144]{2,1,0:T(2,128)(2,1)}), bf16[8,2,6144]{2,1,0:T(2,128)(2,1)}, u32[]{:S(2)}, u32[]{:S(2)}) async-start(bf16[8,2,6144]{2,1,0:T(2,128)(2,1)} %reshape.291), calls=%async_computation.3 | async-start | bytes 393216 | tf_op jit(solution)/shard_map/all_to_all | solution.py:87
  103.3 4.1 copy-start.10
  107.3 0.9 copy-start.11
  117.9 20.3 %copy-start.9 = (bf16[64,2,8,64]{3,2,1,0:T(8,128)(2,1)S(1)}, bf16[64,2,8,64]{3,2,1,0:T(8,128)(2,1)}, u32[]{:S(2)}) copy-start(bf16[64,2,8,64]{3,2,1,0:T(8,128)(2,1)} %reshape.283) | copy-start | bytes 393220
  119.8 14.1 %all-to-all-start.4 = ((bf16[128,8,160]{0,2,1:T(8,128)(2,1)}), bf16[128,8,160]{0,2,1:T(8,128)(2,1)}, u32[]{:S(2)}, u32[]{:S(2)}) async-start(bf16[128,8,160]{0,2,1:T(8,128)(2,1)} %bitcast.172), calls=%async_computation.4 | async-start | bytes 655360 | tf_op jit(solution)/shard_map/all_to_all | solution.py:103
  134.0 21.4 %all-to-all-start.2 = ((bf16[3,512,1,192]{3,0,2,1:T(4,128)(2,1)}), bf16[3,512,1,192]{3,0,2,1:T(4,128)(2,1)}, u32[]{:S(2)}, u32[]{:S(2)}) async-start(bf16[3,512,1,192]{3,0,2,1:T(4,128)(2,1)} %copy.68), calls=%async_computation.2 | async-start | bytes 2097152 | tf_op jit(solution)/shard_map/all_to_all | solution.py:86
  138.2 300.3 %all-reduce.2.cloned.1.call-start = ((), (), s32[]{:S(2)}) async-start(), calls=%async_computation.6 | async-start | bytes 1638400 | tf_op jit(solution)/shard_map/psum | solution.py:111
  143.9 3.4 copy-start.8
  150.3 10.3 %copy-start.6 = (bf16[1,128,512]{2,1,0:T(8,128)(2,1)S(1)}, bf16[1,128,512]{2,1,0:T(8,128)(2,1)}, u32[]{:S(2)}) copy-start(bf16[1,128,512]{2,1,0:T(8,128)(2,1)} %stack.26) | copy-start | bytes 393220
  150.3 10.3 %copy-start.7 = (bf16[1,128,512]{2,1,0:T(8,128)(2,1)S(1)}, bf16[1,128,512]{2,1,0:T(8,128)(2,1)}, u32[]{:S(2)}) copy-start(bf16[1,128,512]{2,1,0:T(8,128)(2,1)} %stack.25) | copy-start | bytes 393220
Sparse Core Ops, SparseCore 0:
  42.7 52.0 all-gather.1
  147.5 291.0 all-reduce.1
where the time goes:
time: 450 us; the launch traced here: 447 us
  waiting for transfers between devices  292 us (65%)
  local copies, waits for them, and re-layouts  52.9 us (12%)
  matrix products  46.3 us (10%)
  starting transfers between devices  29.5 us (7%)
  between operations  14.9 us (3%)
  other arithmetic  11.9 us (3%)
    psum x1, waiting for transfers between devices, on_device(): grad_rows = lax.psum(grad_rows, 'scene')  276 us
  transfers between devices with their start and end apart: 7, of which 4 were waited for; matrix products, arithmetic and copies ran while one was open for 23% of the time, Pallas kernels for 0%

commit v1 on v0

--- a/solution.py
+++ b/solution.py
@@ -108,8 +108,16 @@
         contract_first,
         preferred_element_type=jnp.float32,
     )
-    grad_rows = lax.psum(grad_rows, "scene")
-    weight_grad = grad_rows * (1.0 / math.sqrt(lax.axis_size("scene") * seq_parts * tok_rows))
+    scenes = lax.axis_size("scene")
+    scale = 1.0 / math.sqrt(scenes * seq_parts * tok_rows)
+    rows = grad_rows.shape[0]
+    per = -(-rows // scenes)
+    padded = jnp.pad(grad_rows, ((0, per * scenes - rows), (0, 0))).astype(jnp.bfloat16)
+    pieces = lax.all_to_all(
+        padded.reshape(scenes, per, width), "scene", split_axis=0, concat_axis=0, tiled=True
+    )
+    part = (jnp.sum(pieces.astype(jnp.float32), axis=0) * scale).astype(jnp.bfloat16)
+    weight_grad = lax.all_gather(part, "scene", axis=0, tiled=True)[:rows].astype(jnp.float32)
     return (d_qkv, weight_grad)
 
 

time: 450 us -> 302 us (0.67)
  waiting for transfers between devices: 292 us -> 30.6 us
  blocking collectives: 0 us -> 70.5 us
  starting transfers between devices: 29.5 us -> 67.7 us
  local copies, waits for them, and re-layouts: 52.9 us -> 58.3 us
    psum x1 -> x0, waiting for transfers between devices: 276 us -> none  [on_device(): grad_rows = lax.psum(grad_rows, 'scene')]
    all_gather x0 -> x1, blocking collectives: none -> 70.5 us  [on_device(): lax.all_gather(part, 'scene', axis=0, tiled=True)[:rows].astype(jnp.float32)]
    all_to_all x0 -> x1, starting transfers between devices: none -> 38.2 us  [on_device(): lax.all_to_all(padded.reshape(scenes, per, width), 'scene', split_axis=0,...]
    all_to_all x0 -> x1, waiting for transfers between devices: none -> 7.68 us  [on_device(): lax.all_to_all(padded.reshape(scenes, per, width), 'scene', split_axis=0,...]
    all_to_all x1, waiting for transfers between devices: 5.06 us -> 11.8 us  [on_device(): lax.all_to_all(view_grads, 'seq', split_axis=1, concat_axis=2, tiled=True)]
  transfers between devices with their start and end apart: 7 -> 7, of which waited for: 4 -> 4; matrix products, arithmetic and copies ran while one was open for 23% -> 34% of each run, Pallas kernels for 0% -> 0%
where the time goes in v1:
time: 302 us; the launch traced here: 300 us
  blocking collectives  70.5 us (23%)
  starting transfers between devices  67.7 us (22%)
  local copies, waits for them, and re-layouts  58.3 us (19%)
  matrix products  45.4 us (15%)
  waiting for transfers between devices  30.6 us (10%)
  between operations  14.9 us (5%)
  other arithmetic  12.4 us (4%)
    all_gather x1, blocking collectives, on_device(): lax.all_gather(part, 'scene', axis=0, tiled=True)[:rows].astype(jnp.float32)  70.5 us
    all_to_all x1, starting transfers between devices, on_device(): lax.all_to_all(padded.reshape(scenes, per, width), 'scene', split_axis=0,...  38.2 us
    all_to_all x1, waiting for transfers between devices, on_device(): lax.all_to_all(view_grads, 'seq', split_axis=1, concat_axis=2, tiled=True)  11.8 us
    all_to_all x1, waiting for transfers between devices, on_device(): lax.all_to_all(attn_flat, 'seq', split_axis=1, concat_axis=0, tiled=True)  7.72 us
    all_to_all x1, waiting for transfers between devices, on_device(): lax.all_to_all(padded.reshape(scenes, per, width), 'scene', split_axis=0,...  7.68 us
    dot_general x4, matrix products, attend_back(): jnp.einsum('blhd,bmhd->bhlm', grad_in, values, preferred_element_type=jnp...  7.68 us
    all_to_all x1, starting transfers between devices, on_device(): lax.all_to_all(grad_view, 'seq', split_axis=2, concat_axis=1, tiled=True)  7.63 us
    unnamed x18, local copies, waits for them, and re-layouts  7.23 us
  transfers between devices with their start and end apart: 7, of which 4 were waited for; matrix products, arithmetic and copies ran while one was open for 34% of the time, Pallas kernels for 0%

profile of v1, /device:TPU:1, one launch (start us, length us, event | category | flops | bytes accessed | tf_op | source)
XLA Modules:
  0.0 300.0 jit_solution(4507799722354917197)
XLA Ops:
  7.2 1.9 copy-done
  9.1 2.2 convolution_convert_fusion.4
  14.6 7.6 %all-to-all-start.1 = ((bf16[1,64,8,192]{3,1,0,2:T(8,128)(2,1)}), bf16[1,64,8,192]{3,1,0,2:T(8,128)(2,1)}, u32[]{:S(2)}, u32[]{:S(2)}) async-start(bf16[1,64,8,192]{3,1,0,2:T(8,128)(2,1)} %copy.63), calls=%async_computation.1 | async-start | bytes 524288 | tf_op jit(solution)/shard_map/all_to_all | solution.py:62
  22.2 3.2 %reshape.280 = bf16[3,64,2,1280]{3,2,1,0:T(2,128)(2,1)} reshape(bf16[3,128,1280]{2,1,0:T(8,128)(2,1)} %param.6) | data formatting | bytes 1966080 | tf_op jit(solution)/shard_map/reshape | solution.py:53
  25.4 2.3 slice.57
  27.7 3.0 reshape.281
  30.7 2.2 copy.61
  32.9 6.6 %all-to-all-start = ((bf16[3,64,8,192]{3,1,0,2:T(8,128)(2,1)}), bf16[3,64,8,192]{3,1,0,2:T(8,128)(2,1)}, u32[]{:S(2)}, u32[]{:S(2)}) async-start(bf16[3,64,8,192]{3,1,0,2:T(8,128)(2,1)} %copy.61), calls=%async_computation | async-start | bytes 1572864 | tf_op jit(solution)/shard_map/all_to_all | solution.py:61
  41.0 2.0 fusion.57
  43.0 1.8 reshape.297
  44.8 1.9 reshape.296
  48.5 4.3 %fusion.58 = (f32[64,8,2]{2,1,0:T(8,128)}, f32[64,8,2,2]{2,3,1,0:T(2,128)}) fusion(pred[2]{0:T(512)(128)(4,1)S(1)} %get-tuple-element.133, bf16[64,2,8,64]{3,2,1,0:T(8,128)(2,1)} %reshape.297, bf16[64,2,8,64]{3,2,1,0:T(8,128)(2,1)} %reshape.296), kind=kOutput, calls=%fused_computation.83 | convolution fusion | flops 270337 | bytes 274434 | tf_op jit(solution)/shard_map/sub | solution.py:20
  52.9 1.9 copy.64
  56.0 2.5 copy.62
  58.5 2.7 reshape.282
  61.2 28.8 %while.14 = (s32[]{:T(128)}, bf16[3,512,64]{1,2,0:T(8,128)(2,1)}, bf16[3,3,512,64]{2,3,0,1:T(8,128)(2,1)}, bf16[3,3,512,64]{2,3,0,1:T(8,128)(2,1)}, bf16[3,512,6...) while((s32[]{:T(128)}, bf16[3,512,64]{1,2,0:T(8,128)(2,1)}, ...), condition=%wide.region_4.5_spmd.clone, body=%wide.region_0.4_spmd.clone.sunk | while | flops 208435712 | bytes 21926172 | solution.py:82
  62.7 1.8 fusion.82
  64.7 1.6 fusion.83
  72.3 1.9 fusion.82
  74.3 1.6 fusion.83
  81.9 1.9 fusion.82
  83.9 1.6 fusion.83
  90.0 1.9 copy.84
  92.5 3.2 %reduce.9 = bf16[512,192]{1,0:T(8,128)(2,1)S(1)} reduce(bf16[512,1,1,192]{3,2,1,0:T(2,128)(2,1)} %bitcast.171, bf16[]{:T(256)} %broadcast.103), dimensions={1,2}, to_apply=%bitcast.122.reduce_sub_computation | reduce | bytes 393218
  96.7 6.6 %all-to-all-start.3 = ((bf16[8,2,6144]{2,1,0:T(2,128)(2,1)}), bf16[8,2,6144]{2,1,0:T(2,128)(2,1)}, u32[]{:S(2)}, u32[]{:S(2)}) async-start(bf16[8,2,6144]{2,1,0:T(2,128)(2,1)} %reshape.299), calls=%async_computation.3 | async-start | bytes 393216 | tf_op jit(solution)/shard_map/all_to_all | solution.py:87
  103.3 4.1 %multiply_reduce_fusion.1 = (f32[64,8,2]{2,1,0:T(8,128)}, f32[64,8,2,2]{2,3,1,0:T(2,128)S(1)}, f32[64,8,2,2]{2,3,1,0:T(2,128)}) fusion(f32[64,8,2,2]{2,3,1,0:T(2,128)} %get-tuple-element.130, f32[64,8,2]{2,1,0:T(8,128)} %get-tuple-element.129, bf16[64,2,8,64]{3,2,1,0:T(8,128)(2,1)} %reshape.298, bf16[64,2,8,64]{3,2,1,0:T(8,128)(2,1)} %reshape.286, ...), kind=kOutput, calls=%fused_computation.60 | convolution fusion | flops 529408 | bytes 294916 | tf_op jit(solution)/shard_map/blhd,bmhd->bhlm/dot_general | solution.py:32
  109.2 2.9 all-to-all-done.3
  112.1 2.0 reshape.300
  116.3 1.7 pad_maximum_fusion
  118.0 1.9 copy.89
  119.8 4.1 %all-to-all-start.4 = ((bf16[128,8,160]{0,2,1:T(8,128)(2,1)}), bf16[128,8,160]{0,2,1:T(8,128)(2,1)}, u32[]{:S(2)}, u32[]{:S(2)}) async-start(bf16[128,8,160]{0,2,1:T(8,128)(2,1)} %bitcast.174), calls=%async_computation.4 | async-start | bytes 655360 | tf_op jit(solution)/shard_map/all_to_all | solution.py:103
  123.9 2.3 copy.68
  126.2 7.7 %all-to-all-done.4 = bf16[128,8,160]{0,2,1:T(8,128)(2,1)} async-done(((bf16[128,8,160]{0,2,1:T(8,128)(2,1)}), bf16[128,8,160]{0,2,1:T(8,128)(2,1)}, u32[]{:S(2)}, u32[]{:S(2)}) %all-to-all-start.4) | async-done | bytes 327712 | tf_op jit(solution)/shard_map/all_to_all | solution.py:103
  133.9 4.2 %all-to-all-start.2 = ((bf16[3,512,1,192]{3,0,2,1:T(4,128)(2,1)}), bf16[3,512,1,192]{3,0,2,1:T(4,128)(2,1)}, u32[]{:S(2)}, u32[]{:S(2)}) async-start(bf16[3,512,1,192]{3,0,2,1:T(4,128)(2,1)} %copy.68), calls=%async_computation.2 | async-start | bytes 2097152 | tf_op jit(solution)/shard_map/all_to_all | solution.py:86
  138.2 2.5 convolution_convert_fusion.3
  141.5 2.0 reshape.288
  143.6 11.8 %all-to-all-done.2 = bf16[3,512,1,192]{3,0,2,1:T(4,128)(2,1)} async-done(((bf16[3,512,1,192]{3,0,2,1:T(4,128)(2,1)}), bf16[3,512,1,192]{3,0,2,1:T(4,128)(2,1)}, u32[]{:S(2)}, u32[]{:S(2)}) %all-to-all-start.2) | async-done | bytes 589856 | tf_op jit(solution)/shard_map/all_to_all | solution.py:86
  155.4 38.2 %all-to-all-start.5 = ((bf16[96,2,1280]{2,1,0:T(2,128)(2,1)}), bf16[96,2,1280]{2,1,0:T(2,128)(2,1)}, u32[]{:S(2)}, u32[]{:S(2)}) async-start(bf16[96,2,1280]{2,1,0:T(2,128)(2,1)} %reshape.288), calls=%async_computation.5 | async-start | bytes 983040 | tf_op jit(solution)/shard_map/all_to_all | solution.py:116
  193.6 1.8 fusion.42
  196.3 2.0 fusion.41
  199.3 2.2 fusion.40
  202.3 1.4 copy.69
  205.0 2.6 concatenate.28
  207.6 2.1 maximum_maximum_fusion
  209.8 7.7 %all-to-all-done.5 = bf16[96,2,1280]{2,1,0:T(2,128)(2,1)} async-done(((bf16[96,2,1280]{2,1,0:T(2,128)(2,1)}), bf16[96,2,1280]{2,1,0:T(2,128)(2,1)}, u32[]{:S(2)}, u32[]{:S(2)}) %all-to-all-start.5) | async-done | bytes 491552 | tf_op jit(solution)/shard_map/all_to_all | solution.py:116
  217.4 1.5 convert_reduce_fusion
  218.9 70.5 %all-gather = bf16[96,2,1280]{2,1,0:T(2,128)(2,1)S(1)} all-gather(bf16[1,2,1280]{2,1,0:T(2,128)(2,1)S(1)} %fusion.54), channel_id=1, replica_groups=mesh['scene'=96,'seq'=8] {'scene'}, dimensions={0}, use_global_device_ids=true | all-gather | bytes 496640 | tf_op jit(solution)/shard_map/all_gather | solution.py:120
  290.6 2.6 reshape.292
  (96 shorter events, 37.0 us)
Async XLA Ops:
  7.2 1.9 copy-start
  11.3 0.7 copy-start.5
  14.6 18.3 %all-to-all-start.1 = ((bf16[1,64,8,192]{3,1,0,2:T(8,128)(2,1)}), bf16[1,64,8,192]{3,1,0,2:T(8,128)(2,1)}, u32[]{:S(2)}, u32[]{:S(2)}) async-start(bf16[1,64,8,192]{3,1,0,2:T(8,128)(2,1)} %copy.63), calls=%async_computation.1 | async-start | bytes 524288 | tf_op jit(solution)/shard_map/all_to_all | solution.py:62
  30.7 17.0 %slice-start = ((bf16[128,1280]{1,0:T(8,128)(2,1)}), bf16[128,512]{1,0:T(8,128)(2,1)S(1)}, s32[]{:S(2)}) async-start(bf16[128,1280]{1,0:T(8,128)(2,1)} %copy-done.5), calls=%async_computation.7 | async-start | bytes 262144 | tf_op jit(solution)/shard_map/slice | solution.py:96
  32.9 23.1 %all-to-all-start = ((bf16[3,64,8,192]{3,1,0,2:T(8,128)(2,1)}), bf16[3,64,8,192]{3,1,0,2:T(8,128)(2,1)}, u32[]{:S(2)}, u32[]{:S(2)}) async-start(bf16[3,64,8,192]{3,1,0,2:T(8,128)(2,1)} %copy.61), calls=%async_computation | async-start | bytes 1572864 | tf_op jit(solution)/shard_map/all_to_all | solution.py:61
  39.6 98.7 %all-gather.3.cloned.1.call-start = ((), (), s32[]{:S(2)}) async-start(), calls=%async_computation.6 | async-start | bytes 2949120 | tf_op jit(solution)/shard_map/all_gather | solution.py:107
  61.2 3.4 %copy-start.3 = (bf16[3,512,64]{1,2,0:T(8,128)(2,1)}, bf16[3,512,64]{1,2,0:T(8,128)(2,1)S(1)}, u32[]{:S(2)}) copy-start(bf16[3,512,64]{1,2,0:T(8,128)(2,1)S(1)} %get-tuple-element.211) | copy-start | bytes 589828 | tf_op jit(solution)/shard_map/while
  62.5 2.1 copy-start.1
  64.7 1.6 copy-start.2
  68.8 2.0 copy-start.4
  70.8 3.4 %copy-start.3 = (bf16[3,512,64]{1,2,0:T(8,128)(2,1)}, bf16[3,512,64]{1,2,0:T(8,128)(2,1)S(1)}, u32[]{:S(2)}) copy-start(bf16[3,512,64]{1,2,0:T(8,128)(2,1)S(1)} %get-tuple-element.211) | copy-start | bytes 589828 | tf_op jit(solution)/shard_map/while
  72.1 2.1 copy-start.1
  74.3 1.6 copy-start.2
  78.4 2.0 copy-start.4
  80.4 3.4 %copy-start.3 = (bf16[3,512,64]{1,2,0:T(8,128)(2,1)}, bf16[3,512,64]{1,2,0:T(8,128)(2,1)S(1)}, u32[]{:S(2)}) copy-start(bf16[3,512,64]{1,2,0:T(8,128)(2,1)S(1)} %get-tuple-element.211) | copy-start | bytes 589828 | tf_op jit(solution)/shard_map/while
  81.7 2.1 copy-start.1
  83.9 1.6 copy-start.2
  88.0 2.0 copy-start.4
  96.7 15.4 %all-to-all-start.3 = ((bf16[8,2,6144]{2,1,0:T(2,128)(2,1)}), bf16[8,2,6144]{2,1,0:T(2,128)(2,1)}, u32[]{:S(2)}, u32[]{:S(2)}) async-start(bf16[8,2,6144]{2,1,0:T(2,128)(2,1)} %reshape.299), calls=%async_computation.3 | async-start | bytes 393216 | tf_op jit(solution)/shard_map/all_to_all | solution.py:87
  103.3 4.1 %copy-start.9 = (bf16[64,2,8,64]{3,2,1,0:T(8,128)(2,1)S(1)}, bf16[64,2,8,64]{3,2,1,0:T(8,128)(2,1)}, u32[]{:S(2)}) copy-start(bf16[64,2,8,64]{3,2,1,0:T(8,128)(2,1)} %reshape.298) | copy-start | bytes 393220
  107.4 0.9 copy-start.10
  119.8 14.1 %all-to-all-start.4 = ((bf16[128,8,160]{0,2,1:T(8,128)(2,1)}), bf16[128,8,160]{0,2,1:T(8,128)(2,1)}, u32[]{:S(2)}, u32[]{:S(2)}) async-start(bf16[128,8,160]{0,2,1:T(8,128)(2,1)} %bitcast.174), calls=%async_computation.4 | async-start | bytes 655360 | tf_op jit(solution)/shard_map/all_to_all | solution.py:103
  133.9 21.5 %all-to-all-start.2 = ((bf16[3,512,1,192]{3,0,2,1:T(4,128)(2,1)}), bf16[3,512,1,192]{3,0,2,1:T(4,128)(2,1)}, u32[]{:S(2)}, u32[]{:S(2)}) async-start(bf16[3,512,1,192]{3,0,2,1:T(4,128)(2,1)} %copy.68), calls=%async_computation.2 | async-start | bytes 2097152 | tf_op jit(solution)/shard_map/all_to_all | solution.py:86
  138.2 55.4 %copy-start.8 = (bf16[64,2,8,64]{3,2,1,0:T(8,128)(2,1)S(1)}, bf16[64,2,8,64]{3,2,1,0:T(8,128)(2,1)}, u32[]{:S(2)}) copy-start(bf16[64,2,8,64]{3,2,1,0:T(8,128)(2,1)} %reshape.286) | copy-start | bytes 393220
  155.4 62.0 %all-to-all-start.5 = ((bf16[96,2,1280]{2,1,0:T(2,128)(2,1)}), bf16[96,2,1280]{2,1,0:T(2,128)(2,1)}, u32[]{:S(2)}, u32[]{:S(2)}) async-start(bf16[96,2,1280]{2,1,0:T(2,128)(2,1)} %reshape.288), calls=%async_computation.5 | async-start | bytes 983040 | tf_op jit(solution)/shard_map/all_to_all | solution.py:116
  202.3 5.3 %copy-start.6 = (bf16[1,128,512]{2,1,0:T(8,128)(2,1)S(1)}, bf16[1,128,512]{2,1,0:T(8,128)(2,1)}, u32[]{:S(2)}) copy-start(bf16[1,128,512]{2,1,0:T(8,128)(2,1)} %stack.26) | copy-start | bytes 393220
  202.3 5.3 %copy-start.7 = (bf16[1,128,512]{2,1,0:T(8,128)(2,1)S(1)}, bf16[1,128,512]{2,1,0:T(8,128)(2,1)}, u32[]{:S(2)}) copy-start(bf16[1,128,512]{2,1,0:T(8,128)(2,1)} %stack.25) | copy-start | bytes 393220
Sparse Core Ops, SparseCore 0:
  42.7 51.9 all-gather.2

commit v2 on v0

v2 whole, which is shorter than its diff:
```python
import functools
import math

import jax
import jax.numpy as jnp
from jax import lax
from jax.experimental import pallas as pl
from jax.experimental.pallas import tpu as pltpu
from jax.sharding import PartitionSpec as P

MESH = pl.DeviceIdType.MESH
F32 = jnp.float32
BF16 = jnp.bfloat16
NT = (((1,), (1,)), ((), ()))
TN = (((0,), (0,)), ((), ()))
NN = (((1,), (0,)), ((), ()))

HD = 64
NY, NX, NZ = 8, 4, 12
GROUPS = 4
HEADS = 3
POS = 64
TV = POS * NY
VIEW_W = 768
CROSS_W = 512
WIDTH = 1280
GW = HEADS * HD
PACK = 640
HALF = WIDTH // 2
BLOCKS = 10
OWNED = 5


def dot(a, b, dims=NN):
    return lax.dot_general(a, b, dims, preferred_element_type=F32)


def kernel(
    vc_ref, qkv_ref, cot_ref, w_ref, d_ref, wg_ref,
    wv, wc, qs, qr, cs, cr, cx, xs, xr, cg, hq, hk, hv, hg, pt, dt, dh, ds, dr, ot,
    ws, wr, wown, x_s, x_r, zown, zs, zr, yb, yr, fc,
    wsem, q_ss, q_rs, c_ss, c_rs, x_ss, x_rs, d_ss, d_rs, own_s, k_ss, k_rs, xx_ss, xx_rs,
    z_ss, z_rs, y_ss, y_rs, za_ss, za_rs, xa_ss, xa_rs, ka_ss, ka_rs,
):
    scene = lax.axis_index("scene")
    y = lax.axis_index("seq")
    c = lax.rem(scene, 2)
    x = lax.rem(lax.div(scene, 2), NX)
    z = lax.div(scene, 2 * NX)
    view = lax.div(y, GROUPS)
    group = lax.rem(y, GROUPS)

    def y_at(d):
        return lax.rem(y + d, NY)

    def z_at(d):
        return lax.rem(z + d, NZ)

    def x_at(d):
        return lax.rem(x + d, NX)

    def to_y(p):
        return {"seq": p}

    def to_scene(zz, xx, cc):
        return {"scene": (zz * NX + xx) * 2 + cc}

    core_peer = to_scene(z, x, 1 - c)

    def remote(src, dst, ssem, rsem, dev):
        return pltpu.make_async_remote_copy(
            src_ref=src, dst_ref=dst, send_sem=ssem, recv_sem=rsem, device_id=dev,
            device_id_type=MESH,
        )

    barrier = pltpu.get_barrier_semaphore()
    peers = [to_y(y_at(d)) for d in range(1, NY)]
    peers += [core_peer]
    peers += [to_scene(z, x_at(d), c) for d in range(1, NX)]
    peers += [to_scene(z_at(d), x, c) for d in range(1, NZ)]
    for peer in peers:
        pl.semaphore_signal(barrier, inc=1, device_id=peer, device_id_type=MESH)
    w_view = pltpu.make_async_copy(
        w_ref.at[pl.ds(pl.multiple_of(group * GW, GW), GW)], wv, wsem.at[0]
    )
    w_cross = pltpu.make_async_copy(w_ref.at[pl.ds(VIEW_W, CROSS_W)], wc, wsem.at[1])
    w_cross.start()
    w_view.start()

    vc = vc_ref[0]
    live = [jnp.where(vc > v, 1.0, 0.0).astype(F32) for v in range(2)]
    my_live = jnp.where(vc > view, 1.0, 0.0).astype(F32)

    row = lax.broadcasted_iota(jnp.int32, (POS, 2 * POS), 0)
    col = lax.broadcasted_iota(jnp.int32, (POS, 2 * POS), 1)
    for v in range(2):
        pick = jnp.where(col == 2 * row + v, 1.0, 0.0).astype(BF16)
        parts = []
        for k in range(3):
            r = dot(pick, qkv_ref[k])
            cx[k, v] = r[:, VIEW_W:]
            parts.append(r[:, :VIEW_W])
        for g in range(GROUPS):
            cols = slice(g * GW, (g + 1) * GW)
            packed = jnp.concatenate(
                [p[:, cols] for p in parts] + [jnp.zeros((POS, PACK - 3 * GW), F32)], axis=1
            )
            qs[v * GROUPS + g] = packed.astype(BF16)
        cs[v] = dot(pick, cot_ref[...]).astype(BF16)

    pl.semaphore_wait(barrier, len(peers))

    def rows_of(ref, p):
        return ref.at[pl.ds(pl.multiple_of(p * POS, POS), POS)]

    def q_copy(d, mine):
        p = y_at(d)
        at = y if mine else p
        return remote(qs.at[p], rows_of(qr, at), q_ss.at[d], q_rs.at[at], to_y(p))

    def c_copy(d, mine):
        p = y_at(d)
        at = y if mine else p
        return remote(
            cs.at[lax.div(p, GROUPS)], rows_of(cr, at), c_ss.at[d], c_rs.at[at], to_y(p)
        )

    def x_copy(d, mine):
        p = y_at(d)
        at = y if mine else p
        return remote(xs.at[p], rows_of(xr, at), x_ss.at[d], x_rs.at[at], to_y(p))

    def d_copy(d, mine):
        p = y_at(d)
        at = y if mine else p
        return remote(rows_of(ds, p), dr.at[at], d_ss.at[d], d_rs.at[at], to_y(p))

    q_own = pltpu.make_async_copy(qs.at[y], rows_of(qr, y), own_s.at[0])
    c_own = pltpu.make_async_copy(cs.at[view], rows_of(cr, y), own_s.at[1])
    x_own = pltpu.make_async_copy(xs.at[y], rows_of(xr, y), own_s.at[2])
    d_own = pltpu.make_async_copy(rows_of(ds, y), dr.at[y], own_s.at[3])

    for d in range(1, NY):
        q_copy(d, True).start()
    q_own.start()
    for d in range(1, NY):
        c_copy(d, True).start()
    c_own.start()

    w_cross.wait()
    same = jnp.where(
        lax.broadcasted_iota(jnp.int32, (CROSS_W, CROSS_W), 0) // HD
        == lax.broadcasted_iota(jnp.int32, (CROSS_W, CROSS_W), 1) // HD,
        1.0,
        0.0,
    ).astype(BF16)

    def head_sum(t):
        hi = t.astype(BF16)
        lo = (t - hi.astype(F32)).astype(BF16)
        return dot(hi, same) + dot(lo, same)

    scale = 1.0 / math.sqrt(HD)
    gs = []
    for v in range(2):
        g = dot(cs[v], wc[...], NT).astype(BF16).astype(F32)
        gs.append(g * live[v])
    dq = []
    dk = [None, None]
    dv = [None, None]
    for a in range(2):
        q = cx[0, a]
        s0 = head_sum(q * cx[1, 0]) * scale
        s1 = head_sum(q * cx[1, 1]) * scale
        s1 = jnp.where(live[1] > 0.5, s1, -1e30)
        m = jnp.maximum(s0, s1)
        e0 = jnp.exp(s0 - m)
        e1 = jnp.exp(s1 - m)
        inv = 1.0 / (e0 + e1)
        p = [e0 * inv, e1 * inv]
        pb = [t.astype(BF16).astype(F32) for t in p]
        out = ((pb[0] * cx[2, 0] + pb[1] * cx[2, 1]) * live[a]).astype(BF16)
        for g in range(GROUPS):
            xs[a * GROUPS + g] = out[:, g * 128 : (g + 1) * 128]
        dp = [head_sum(gs[a] * cx[2, b]) for b in range(2)]
        mean = p[0] * dp[0] + p[1] * dp[1]
        grad = [p[b] * (dp[b] - mean) * scale for b in range(2)]
        dq.append(grad[0] * cx[1, 0] + grad[1] * cx[1, 1])
        for b in range(2):
            tk = grad[b] * q
            tv = pb[b] * gs[a]
            dk[b] = tk if dk[b] is None else dk[b] + tk
            dv[b] = tv if dv[b] is None else dv[b] + tv
    for d in range(1, NY):
        x_copy(d, True).start()
    x_own.start()
    for v in range(2):
        cg[0, v] = dq[v].astype(BF16)
        cg[1, v] = dk[v].astype(BF16)
        cg[2, v] = dv[v].astype(BF16)

    for d in range(1, NY):
        q_copy(d, False).wait_recv()
    q_own.wait()
    packed = qr[...]
    for h in range(HEADS):
        hq[h] = packed[:, h * HD : (h + 1) * HD]
        hk[h] = packed[:, GW + h * HD : GW + (h + 1) * HD]
        hv[h] = packed[:, 2 * GW + h * HD : 2 * GW + (h + 1) * HD]
    w_view.wait()
    for d in range(1, NY):
        c_copy(d, False).wait_recv()
    c_own.wait()
    g_all = (dot(cr[...], wv[...], NT).astype(BF16).astype(F32) * my_live).astype(BF16)
    for h in range(HEADS):
        hg[h] = g_all[:, h * HD : (h + 1) * HD]

    chunk = 128

    def one_head(h, carry):
        k = hk[h]
        v = hv[h]
        for i in range(TV // chunk):
            at = slice(i * chunk, (i + 1) * chunk)
            s = dot(k, hq[h, at, :], NT) * scale
            e = jnp.exp(s - jnp.max(s, axis=0, keepdims=True))
            p = e * (1.0 / jnp.sum(e, axis=0, keepdims=True))
            dp = dot(v, hg[h, at, :], NT)
            mean = jnp.sum(p * dp, axis=0, keepdims=True)
            pt[:, at] = p.astype(BF16)
            dt[:, at] = (p * (dp - mean) * scale).astype(BF16)
        probs = pt[...]
        grads = dt[...]
        ot[pl.ds(pl.multiple_of(h * HD, HD), HD), :] = (dot(v, probs, TN) * my_live).astype(BF16)
        dh[h, 0] = dot(k, grads, TN).T
        dh[h, 1] = dot(grads, hq[h])
        dh[h, 2] = dot(probs, hg[h])
        return carry

    lax.fori_loop(0, HEADS, one_head, 0)
    ds[...] = jnp.concatenate(
        [dh[h, k] for k in range(3) for h in range(HEADS)]
        + [jnp.zeros((TV, PACK - 3 * GW), F32)],
        axis=1,
    ).astype(BF16)
    for d in range(1, NY):
        d_copy(d, True).start()
    d_own.start()

    for d in range(1, NY):
        x_copy(d, False).wait_recv()
    x_own.wait()

    def partial(cc):
        cols = pl.ds(pl.multiple_of(cc * HALF, HALF), HALF)
        return jnp.concatenate(
            [dot(ot[...], cr[:, cols]), dot(xr[...], cr[:, cols], TN)], axis=0
        )

    ws[...] = partial(1 - c).astype(BF16)
    k_copy = remote(ws, wr, k_ss, k_rs, core_peer)
    k_copy.start()
    own = partial(c)
    k_copy.wait_recv()
    wown[...] = (own + wr[...].astype(F32)).reshape(BLOCKS, NX, 8, HALF)

    for i in range(NX):
        x_s[i] = wown[:, i].reshape(BLOCKS * 8, HALF).astype(BF16)

    def xx_copy(d, mine):
        p = x_at(d)
        at = x if mine else p
        return remote(x_s.at[p], x_r.at[at], xx_ss.at[d], xx_rs.at[at], to_scene(z, p, c))

    for d in range(1, NX):
        xx_copy(d, True).start()
    total = wown[:, x].reshape(BLOCKS * 8, HALF)
    for d in range(1, NX):
        xx_copy(d, False).wait_recv()
        total = total + x_r[x_at(d)].astype(F32)
    zown[:BLOCKS] = total.reshape(BLOCKS, 8, HALF)
    for j in range(BLOCKS):
        zs[j] = total[8 * j : 8 * j + 8].astype(BF16)

    def local_block(zz):
        late = lax.div(zz, 6)
        return (1 - late) * zz + late * (6 + lax.rem(zz + 24 - 4 * group, 6))

    def z_copy(d, mine):
        p = z_at(d)
        at = z if mine else p
        return remote(zs.at[local_block(p)], zr.at[at], z_ss.at[d], z_rs.at[at], to_scene(p, x, c))

    for d in range(1, NZ):

        @pl.when(local_block(z_at(d)) < BLOCKS)
        def _():
            z_copy(d, True).start()

    late = lax.div(z, 6)
    mine_at = local_block(z)
    blk = (1 - late) * (6 * group + mine_at) + late * (18 + 4 * group + mine_at)
    owner = lax.div(blk, OWNED)
    y_copy = remote(yb, yr.at[view], y_ss, y_rs.at[view], to_y(owner))
    y_own = pltpu.make_async_copy(yb, yr.at[view], own_s.at[4])
    away = jnp.logical_and(mine_at < BLOCKS, owner != y)
    here = jnp.logical_and(mine_at < BLOCKS, owner == y)

    @pl.when(mine_at < BLOCKS)
    def _():
        acc = zown[mine_at]
        for d in range(1, NZ):
            z_copy(d, False).wait_recv()
            acc = acc + zr[z_at(d)].astype(F32)
        yb[...] = acc.astype(BF16)

    @pl.when(away)
    def _():
        y_copy.start()

    @pl.when(here)
    def _():
        y_own.start()

    tokens = TV * 2 * NZ * NX * 2
    slots = []
    for i in range(OWNED):
        b = y * OWNED + i
        high = lax.div(b, 24)
        rest = b - 24 * high
        src_group = (1 - high) * lax.div(rest, 6) + high * lax.div(rest, 4)
        src_z = 6 * high + lax.rem(b, 6)
        slots.append((src_group, src_z))

    def za_copy(i, d):
        piece = fc.at[c, x, i]
        return remote(piece, piece, za_ss.at[d], za_rs.at[i], to_scene(z_at(d), x, c))

    for i, (src_group, src_z) in enumerate(slots):

        @pl.when(src_z == z)
        def _():
            for v in range(2):
                src_y = v * GROUPS + src_group

                @pl.when(src_y != y)
                def _():
                    remote(yb, yr.at[v], y_ss, y_rs.at[v], to_y(src_y)).wait_recv()

                @pl.when(src_y == y)
                def _():
                    pltpu.make_async_copy(yb, yr.at[v], own_s.at[4]).wait()

            both = yr[0].astype(F32) + yr[1].astype(F32)
            fc[c, x, i] = (both * (1.0 / math.sqrt(tokens))).astype(BF16)
            for d in range(1, NZ):
                za_copy(i, d).start()

    for d in range(1, NY):
        d_copy(d, False).wait_recv()
    d_own.wait()
    trow = lax.broadcasted_iota(jnp.int32, (2 * POS, POS), 0)
    tcol = lax.broadcasted_iota(jnp.int32, (2 * POS, POS), 1)
    place = [jnp.where(trow == 2 * tcol + v, 1.0, 0.0).astype(BF16) for v in range(2)]
    for k in range(3):
        cols = slice(k * GW, (k + 1) * GW)
        acc = None
        for v in range(2):
            view_part = jnp.concatenate(
                [dr[v * GROUPS + g][:, cols].astype(F32) for g in range(GROUPS)], axis=1
            ).astype(BF16)
            full = jnp.concatenate([view_part, cg[k, v]], axis=1)
            t = dot(place[v], full)
            acc = t if acc is None else acc + t
        d_ref[k] = acc.astype(BF16)

    for i, (_, src_z) in enumerate(slots):

        @pl.when(src_z != z)
        def _():
            za_copy(i, 1).wait_recv()

    def xa_copy(d, mine):
        p = x_at(d)
        piece = fc.at[c, x if mine else p]
        return remote(piece, piece, xa_ss.at[d], xa_rs.at[x if mine else p], to_scene(z, p, c))

    for d in range(1, NX):
        xa_copy(d, True).start()
    for d in range(1, NX):
        xa_copy(d, False).wait_recv()
    ka_copy = remote(fc.at[c], fc.at[c], ka_ss, ka_rs, core_peer)
    ka_copy.start()
    remote(fc.at[1 - c], fc.at[1 - c], ka_ss, ka_rs, core_peer).wait_recv()
    for cc in range(2):
        for xx in range(NX):
            for i in range(OWNED):
                at = 32 * i + 8 * xx
                wg_ref[at : at + 8, cc * HALF : (cc + 1) * HALF] = fc[cc, xx, i].astype(F32)

    for d in range(1, NY):
        q_copy(d, True).wait_send()
        c_copy(d, True).wait_send()
        x_copy(d, True).wait_send()
        d_copy(d, True).wait_send()
    k_copy.wait_send()
    for d in range(1, NX):
        xx_copy(d, True).wait_send()
        xa_copy(d, True).wait_send()
    for d in range(1, NZ):

        @pl.when(local_block(z_at(d)) < BLOCKS)
        def _():
            z_copy(d, True).wait_send()

    @pl.when(away)
    def _():
        y_copy.wait_send()

    for i, (_, src_z) in enumerate(slots):

        @pl.when(src_z == z)
        def _():
            for d in range(1, NZ):
                za_copy(i, d).wait_send()

    ka_copy.wait_send()


def on_device(qkv, view_counts, out_weight, out_cotangent):
    vmem = pl.BlockSpec(memory_space=pltpu.VMEM)
    V = pltpu.VMEM
    S = pltpu.SemaphoreType.DMA
    return pl.pallas_call(
        kernel,
        out_shape=(
            jax.ShapeDtypeStruct((3, 2 * POS, WIDTH), BF16),
            jax.ShapeDtypeStruct((WIDTH // NY, WIDTH), F32),
        ),
        in_specs=[
            pl.BlockSpec(memory_space=pltpu.SMEM), vmem, vmem, pl.BlockSpec(memory_space=pl.ANY),
        ],
        out_specs=(vmem, vmem),
        scratch_shapes=[
            V((GW, WIDTH), BF16), V((CROSS_W, WIDTH), BF16),
            V((NY, POS, PACK), BF16), V((TV, PACK), BF16),
            V((2, POS, WIDTH), BF16), V((TV, WIDTH), BF16),
            V((3, 2, POS, CROSS_W), F32),
            V((NY, POS, 128), BF16), V((TV, 128), BF16),
            V((3, 2, POS, CROSS_W), BF16),
            V((HEADS, TV, HD), BF16), V((HEADS, TV, HD), BF16),
            V((HEADS, TV, HD), BF16), V((HEADS, TV, HD), BF16),
            V((TV, TV), BF16), V((TV, TV), BF16),
            V((HEADS, 3, TV, HD), F32),
            V((TV, PACK), BF16), V((NY, POS, PACK), BF16),
            V((GW, TV), BF16),
            V((320, HALF), BF16), V((320, HALF), BF16), V((BLOCKS, NX, 8, HALF), F32),
            V((NX, BLOCKS * 8, HALF), BF16), V((NX, BLOCKS * 8, HALF), BF16),
            V((NZ, 8, HALF), F32), V((NZ, 8, HALF), BF16), V((NZ, 8, HALF), BF16),
            V((8, HALF), BF16), V((2, 8, HALF), BF16), V((2, NX, OWNED, 8, HALF), BF16),
            S((2,)), S((NY,)), S((NY,)), S((NY,)), S((NY,)), S((NY,)), S((NY,)),
            S((NY,)), S((NY,)), S((5,)), S, S, S((NX,)), S((NX,)),
            S((NZ,)), S((NZ,)), S, S((2,)), S((NZ,)), S((OWNED,)), S((NX,)), S((NX,)), S, S,
        ],
        compiler_params=pltpu.CompilerParams(
            collective_id=0, has_side_effects=True, vmem_limit_bytes=60 * 1024 * 1024
        ),
        name="layer",
    )(view_counts, qkv, out_cotangent, out_weight)


def solution(mesh):
    in_specs = (P(None, ("scene", "seq"), None), P("scene"), P(), P(("scene", "seq"), None))
    out_specs = (P(None, ("scene", "seq"), None), P("seq", None))
    return jax.shard_map(
        on_device, mesh=mesh, in_specs=in_specs, out_specs=out_specs, check_vma=False
    )
```

time: 450 us -> 114 us (0.25)
  waiting for transfers between devices: 292 us -> 0 us
  Pallas kernels: 0 us -> 109 us
  local copies, waits for them, and re-layouts: 52.9 us -> 4.3 us
  matrix products: 46.3 us -> 0 us
  starting transfers between devices: 29.5 us -> 0 us
  between operations: 14.9 us -> 1.28 us
  other arithmetic: 11.9 us -> 0 us
    psum x1 -> x0, waiting for transfers between devices: 276 us -> none  [on_device(): grad_rows = lax.psum(grad_rows, 'scene')]
    pallas_call x0 -> x1, Pallas kernels: none -> 109 us  [on_device(): pl.pallas_call(kernel, out_shape=(jax.ShapeDtypeStruct((3, 2 * POS, WIDTH...]
    dot_general x25 -> x0, matrix products: 42 us -> none  [the longest x4 7.68 us: attend_back(): jnp.einsum('blhd,bmhd->bhlm', grad_in, values, preferred_element_type=jnp...]
    all_to_all x5 -> x0, starting transfers between devices: 29.2 us -> none  [the longest x1 7.63 us: on_device(): lax.all_to_all(grad_view, 'seq', split_axis=2, concat_axis=1, tiled=True)]
    reshape x10 -> x0, local copies, waits for them, and re-layouts: 19.4 us -> none  [the longest x2 5.19 us: on_device(): local[..., :view_width].reshape(3, places, VMAX * groups, group_width)]
    all_to_all x5 -> x0, waiting for transfers between devices: 15.6 us -> none  [the longest x1 7.71 us: on_device(): lax.all_to_all(attn_flat, 'seq', split_axis=1, concat_axis=0, tiled=True)]
    all_to_all x5 -> x0, local copies, waits for them, and re-layouts: 7.2 us -> none  [the longest x2 2.65 us: on_device(): lax.all_to_all(view_grads, 'seq', split_axis=1, concat_axis=2, tiled=True)]
    concatenate x4 -> x0, local copies, waits for them, and re-layouts: 6.29 us -> none  [the longest x3 3.74 us: on_device(): jnp.concatenate([out_home, cross_flat], axis=-1).reshape(tok_rows, width)]
  transfers between devices with their start and end apart: 7 -> 0, of which waited for: 4 -> 0; matrix products, arithmetic and copies ran while one was open for 23% -> 0% of each run, Pallas kernels for 0% -> 0%
where the time goes in v2:
time: 114 us
  Pallas kernels  109 us (96%)
  local copies, waits for them, and re-layouts  4.3 us (4%)
  between operations  1.28 us (1%)
    pallas_call x1, Pallas kernels, on_device(): pl.pallas_call(kernel, out_shape=(jax.ShapeDtypeStruct((3, 2 * POS, WIDTH...  109 us
    unnamed x2, local copies, waits for them, and re-layouts  4.3 us

profile of v2, /device:TPU:1, one launch (start us, length us, event | category | flops | bytes accessed | tf_op | source)
XLA Modules:
  0.0 114.1 jit_solution(9505627077599608123)
XLA Ops:
  1.3 108.5 %layer.1 = (bf16[3,128,1280]{2,1,0:T(8,128)(2,1)}, f32[160,1280]{1,0:T(8,128)}) custom-call(s32[1]{0:T(128)S(6)} %copy.8.vc_ref, bf16[3,128,1280]{2,1,0:T(8,128)(2,1)} %qkv_ref.1, bf16[128,1280]{1,0:T(8,128)(2,1)} %cot_ref.1, bf16[1280,1280]{1,0:T(8,128)(2,1)} %w_ref.1), custom_call_target="tpu_custom_call" | custom-call | tf_op jit(solution)/shard_map/layer/pallas_call | solution.py:434
  109.8 2.2 %copy.9 = bf16[3,128,1280]{2,1,0:T(8,128)(2,1)} copy(bf16[3,128,1280]{2,1,0:T(8,128)(2,1)} %get-tuple-element.4) | data formatting | bytes 1966080
  112.0 2.1 %copy.10 = f32[160,1280]{1,0:T(8,128)} copy(f32[160,1280]{1,0:T(8,128)} %get-tuple-element.5) | data formatting | bytes 1638400

commit v3 on v2

--- a/solution.py
+++ b/solution.py
@@ -37,9 +37,9 @@
 
 def kernel(
     vc_ref, qkv_ref, cot_ref, w_ref, d_ref, wg_ref,
-    wv, wc, qs, qr, cs, cr, cx, xs, xr, cg, hq, hk, hv, hg, pt, dt, dh, ds, dr, ot,
+    wv, wc, qs, qr, cs, cr, cx, xs, xr, cg, hq, hk, hv, hg, pf, pr, dt, da, db, dc, ra, rb, rc, ot,
     ws, wr, wown, x_s, x_r, zown, zs, zr, yb, yr, fc,
-    wsem, q_ss, q_rs, c_ss, c_rs, x_ss, x_rs, d_ss, d_rs, own_s, k_ss, k_rs, xx_ss, xx_rs,
+    wsem, q_ss, q_rs, c_ss, c_rs, x_ss, x_rs, da_ss, da_rs, db_ss, db_rs, dc_ss, dc_rs, own_s, k_ss, k_rs, xx_ss, xx_rs,
     z_ss, z_rs, y_ss, y_rs, za_ss, za_rs, xa_ss, xa_rs, ka_ss, ka_rs,
 ):
     scene = lax.axis_index("scene")
@@ -106,7 +106,6 @@
                 [p[:, cols] for p in parts] + [jnp.zeros((POS, PACK - 3 * GW), F32)], axis=1
             )
             qs[v * GROUPS + g] = packed.astype(BF16)
-        cs[v] = dot(pick, cot_ref[...]).astype(BF16)
 
     pl.semaphore_wait(barrier, len(peers))
 
@@ -130,19 +129,29 @@
         at = y if mine else p
         return remote(xs.at[p], rows_of(xr, at), x_ss.at[d], x_rs.at[at], to_y(p))
 
-    def d_copy(d, mine):
+    returned = [(da, ra, da_ss, da_rs), (db, rb, db_ss, db_rs), (dc, rc, dc_ss, dc_rs)]
+
+    def d_copy(n, d, mine):
+        src, dst, ssem, rsem = returned[n]
         p = y_at(d)
         at = y if mine else p
-        return remote(rows_of(ds, p), dr.at[at], d_ss.at[d], d_rs.at[at], to_y(p))
+        return remote(rows_of(src, p), dst.at[at], ssem.at[d], rsem.at[at], to_y(p))
+
+    d_own = [
+        pltpu.make_async_copy(rows_of(src, y), dst.at[y], own_s.at[5 + n])
+        for n, (src, dst, _, _) in enumerate(returned)
+    ]
 
     q_own = pltpu.make_async_copy(qs.at[y], rows_of(qr, y), own_s.at[0])
     c_own = pltpu.make_async_copy(cs.at[view], rows_of(cr, y), own_s.at[1])
     x_own = pltpu.make_async_copy(xs.at[y], rows_of(xr, y), own_s.at[2])
-    d_own = pltpu.make_async_copy(rows_of(ds, y), dr.at[y], own_s.at[3])
 
     for d in range(1, NY):
         q_copy(d, True).start()
     q_own.start()
+    for v in range(2):
+        pick = jnp.where(col == 2 * row + v, 1.0, 0.0).astype(BF16)
+        cs[v] = dot(pick, cot_ref[...]).astype(BF16)
     for d in range(1, NY):
         c_copy(d, True).start()
     c_own.start()
@@ -207,17 +216,9 @@
         hq[h] = packed[:, h * HD : (h + 1) * HD]
         hk[h] = packed[:, GW + h * HD : GW + (h + 1) * HD]
         hv[h] = packed[:, 2 * GW + h * HD : 2 * GW + (h + 1) * HD]
-    w_view.wait()
-    for d in range(1, NY):
-        c_copy(d, False).wait_recv()
-    c_own.wait()
-    g_all = (dot(cr[...], wv[...], NT).astype(BF16).astype(F32) * my_live).astype(BF16)
-    for h in range(HEADS):
-        hg[h] = g_all[:, h * HD : (h + 1) * HD]
-
     chunk = 128
 
-    def one_head(h, carry):
+    def forward(h, carry):
         k = hk[h]
         v = hv[h]
         for i in range(TV // chunk):
@@ -225,28 +226,28 @@
             s = dot(k, hq[h, at, :], NT) * scale
             e = jnp.exp(s - jnp.max(s, axis=0, keepdims=True))
             p = e * (1.0 / jnp.sum(e, axis=0, keepdims=True))
+            pf[h, :, at] = p
+            pr[h, :, at] = p.astype(BF16)
+        ot[pl.ds(pl.multiple_of(h * HD, HD), HD), :] = (dot(v, pr[h], TN) * my_live).astype(BF16)
+        return carry
+
+    lax.fori_loop(0, HEADS, forward, 0)
+
+    def backward(h):
+        k = hk[h]
+        v = hv[h]
+        for i in range(TV // chunk):
+            at = slice(i * chunk, (i + 1) * chunk)
+            p = pf[h, :, at]
             dp = dot(v, hg[h, at, :], NT)
             mean = jnp.sum(p * dp, axis=0, keepdims=True)
-            pt[:, at] = p.astype(BF16)
             dt[:, at] = (p * (dp - mean) * scale).astype(BF16)
-        probs = pt[...]
         grads = dt[...]
-        ot[pl.ds(pl.multiple_of(h * HD, HD), HD), :] = (dot(v, probs, TN) * my_live).astype(BF16)
-        dh[h, 0] = dot(k, grads, TN).T
-        dh[h, 1] = dot(grads, hq[h])
-        dh[h, 2] = dot(probs, hg[h])
-        return carry
-
-    lax.fori_loop(0, HEADS, one_head, 0)
-    ds[...] = jnp.concatenate(
-        [dh[h, k] for k in range(3) for h in range(HEADS)]
-        + [jnp.zeros((TV, PACK - 3 * GW), F32)],
-        axis=1,
-    ).astype(BF16)
-    for d in range(1, NY):
-        d_copy(d, True).start()
-    d_own.start()
-
+        return dot(k, grads, TN).T, dot(grads, hq[h]), dot(pr[h], hg[h])
+
+    for d in range(1, NY):
+        c_copy(d, False).wait_recv()
+    c_own.wait()
     for d in range(1, NY):
         x_copy(d, False).wait_recv()
     x_own.wait()
@@ -260,10 +261,21 @@
     ws[...] = partial(1 - c).astype(BF16)
     k_copy = remote(ws, wr, k_ss, k_rs, core_peer)
     k_copy.start()
-    own = partial(c)
+    wown[...] = partial(c).reshape(BLOCKS, NX, 8, HALF)
+
+    w_view.wait()
+    g_all = (dot(cr[...], wv[...], NT).astype(BF16).astype(F32) * my_live).astype(BF16)
+    for h in range(HEADS):
+        hg[h] = g_all[:, h * HD : (h + 1) * HD]
+    dq0, dk0, dv0 = backward(0)
+    da[...] = jnp.concatenate([dq0, dk0], axis=1).astype(BF16)
+    db[:, 2 * HD : 3 * HD] = dv0.astype(BF16)
+    for d in range(1, NY):
+        d_copy(0, d, True).start()
+    d_own[0].start()
+
     k_copy.wait_recv()
-    wown[...] = (own + wr[...].astype(F32)).reshape(BLOCKS, NX, 8, HALF)
-
+    wown[...] = wown[...] + wr[...].astype(F32).reshape(BLOCKS, NX, 8, HALF)
     for i in range(NX):
         x_s[i] = wown[:, i].reshape(BLOCKS * 8, HALF).astype(BF16)
 
@@ -274,6 +286,12 @@
 
     for d in range(1, NX):
         xx_copy(d, True).start()
+    dq1, dk1, dv1 = backward(1)
+    db[:, : 2 * HD] = jnp.concatenate([dq1, dk1], axis=1).astype(BF16)
+    db[:, 3 * HD :] = dv1.astype(BF16)
+    for d in range(1, NY):
+        d_copy(1, d, True).start()
+    d_own[1].start()
     total = wown[:, x].reshape(BLOCKS * 8, HALF)
     for d in range(1, NX):
         xx_copy(d, False).wait_recv()
@@ -296,6 +314,12 @@
         @pl.when(local_block(z_at(d)) < BLOCKS)
         def _():
             z_copy(d, True).start()
+
+    dq2, dk2, dv2 = backward(2)
+    dc[...] = jnp.concatenate([dq2, dk2, dv2, jnp.zeros((TV, HD), F32)], axis=1).astype(BF16)
+    for d in range(1, NY):
+        d_copy(2, d, True).start()
+    d_own[2].start()
 
     late = lax.div(z, 6)
     mine_at = local_block(z)
@@ -356,18 +380,28 @@
             for d in range(1, NZ):
                 za_copy(i, d).start()
 
-    for d in range(1, NY):
-        d_copy(d, False).wait_recv()
-    d_own.wait()
+    for n in range(3):
+        for d in range(1, NY):
+            d_copy(n, d, False).wait_recv()
+        d_own[n].wait()
     trow = lax.broadcasted_iota(jnp.int32, (2 * POS, POS), 0)
     tcol = lax.broadcasted_iota(jnp.int32, (2 * POS, POS), 1)
     place = [jnp.where(trow == 2 * tcol + v, 1.0, 0.0).astype(BF16) for v in range(2)]
+    homes = [
+        [(ra, 0), (rb, 0), (rc, 0)],
+        [(ra, HD), (rb, HD), (rc, HD)],
+        [(rb, 2 * HD), (rb, 3 * HD), (rc, 2 * HD)],
+    ]
     for k in range(3):
-        cols = slice(k * GW, (k + 1) * GW)
         acc = None
         for v in range(2):
             view_part = jnp.concatenate(
-                [dr[v * GROUPS + g][:, cols].astype(F32) for g in range(GROUPS)], axis=1
+                [
+                    ref[v * GROUPS + g][:, lane : lane + HD].astype(F32)
+                    for g in range(GROUPS)
+                    for ref, lane in homes[k]
+                ],
+                axis=1,
             ).astype(BF16)
             full = jnp.concatenate([view_part, cg[k, v]], axis=1)
             t = dot(place[v], full)
@@ -402,7 +436,8 @@
         q_copy(d, True).wait_send()
         c_copy(d, True).wait_send()
         x_copy(d, True).wait_send()
-        d_copy(d, True).wait_send()
+        for n in range(3):
+            d_copy(n, d, True).wait_send()
     k_copy.wait_send()
     for d in range(1, NX):
         xx_copy(d, True).wait_send()
@@ -438,7 +473,7 @@
             jax.ShapeDtypeStruct((WIDTH // NY, WIDTH), F32),
         ),
         in_specs=[
-            pl.BlockSpec(memory_space=pltpu.SMEM), vmem, vmem, pl.BlockSpec(memory_space=pl.ANY),
+            pl.BlockSpec(memory_space=pltpu.SMEM), vmem, vmem, pl.BlockSpec(memory_space=pltpu.HBM),
         ],
         out_specs=(vmem, vmem),
         scratch_shapes=[
@@ -450,20 +485,20 @@
             V((3, 2, POS, CROSS_W), BF16),
             V((HEADS, TV, HD), BF16), V((HEADS, TV, HD), BF16),
             V((HEADS, TV, HD), BF16), V((HEADS, TV, HD), BF16),
-            V((TV, TV), BF16), V((TV, TV), BF16),
-            V((HEADS, 3, TV, HD), F32),
-            V((TV, PACK), BF16), V((NY, POS, PACK), BF16),
+            V((HEADS, TV, TV), F32), V((HEADS, TV, TV), BF16), V((TV, TV), BF16),
+            V((TV, 128), BF16), V((TV, 256), BF16), V((TV, 256), BF16),
+            V((NY, POS, 128), BF16), V((NY, POS, 256), BF16), V((NY, POS, 256), BF16),
             V((GW, TV), BF16),
             V((320, HALF), BF16), V((320, HALF), BF16), V((BLOCKS, NX, 8, HALF), F32),
             V((NX, BLOCKS * 8, HALF), BF16), V((NX, BLOCKS * 8, HALF), BF16),
             V((NZ, 8, HALF), F32), V((NZ, 8, HALF), BF16), V((NZ, 8, HALF), BF16),
             V((8, HALF), BF16), V((2, 8, HALF), BF16), V((2, NX, OWNED, 8, HALF), BF16),
             S((2,)), S((NY,)), S((NY,)), S((NY,)), S((NY,)), S((NY,)), S((NY,)),
-            S((NY,)), S((NY,)), S((5,)), S, S, S((NX,)), S((NX,)),
+            S((NY,)), S((NY,)), S((NY,)), S((NY,)), S((NY,)), S((NY,)), S((8,)), S, S, S((NX,)), S((NX,)),
             S((NZ,)), S((NZ,)), S, S((2,)), S((NZ,)), S((OWNED,)), S((NX,)), S((NX,)), S, S,
         ],
         compiler_params=pltpu.CompilerParams(
-            collective_id=0, has_side_effects=True, vmem_limit_bytes=60 * 1024 * 1024
+            collective_id=0, has_side_effects=True, vmem_limit_bytes=30 * 1024 * 1024
         ),
         name="layer",
     )(view_counts, qkv, out_cotangent, out_weight)

time: 114 us -> 109 us (0.956)
  Pallas kernels: 109 us -> 102 us
  local copies, waits for them, and re-layouts: 4.3 us -> 5.93 us
    pallas_call x1, Pallas kernels: 109 us -> 102 us  [on_device(): pl.pallas_call(kernel, out_shape=(jax.ShapeDtypeStruct((3, 2 * POS, WIDTH...]
    unnamed x2 -> x8, local copies, waits for them, and re-layouts: 4.3 us -> 5.93 us
where the time goes in v3:
time: 109 us
  Pallas kernels  102 us (94%)
  local copies, waits for them, and re-layouts  5.93 us (5%)
  between operations  1.29 us (1%)
    pallas_call x1, Pallas kernels, on_device(): pl.pallas_call(kernel, out_shape=(jax.ShapeDtypeStruct((3, 2 * POS, WIDTH...  102 us
    unnamed x8, local copies, waits for them, and re-layouts  5.93 us

profile of v3, /device:TPU:1, one launch (start us, length us, event | category | flops | bytes accessed | tf_op | source)
XLA Modules:
  0.0 108.9 jit_solution(2261382715140336492)
XLA Ops:
  1.3 0.0 copy-start
  1.3 1.9 %copy-done = bf16[1280,1280]{1,0:T(8,128)(2,1)S(1)} copy-done((bf16[1280,1280]{1,0:T(8,128)(2,1)S(1)}, bf16[1280,1280]{1,0:T(8,128)(2,1)}, u32[]{:S(2)}) %copy-start) | copy-done | bytes 3276824
  3.2 0.0 copy-start.1
  3.2 1.2 %copy-done.1 = bf16[3,128,1280]{2,1,0:T(8,128)(2,1)S(1)} copy-done((bf16[3,128,1280]{2,1,0:T(8,128)(2,1)S(1)}, bf16[3,128,1280]{2,1,0:T(8,128)(2,1)}, u32[]{:S(2)}) %copy-start.1) | copy-done | bytes 983064
  4.4 0.0 copy-start.2
  4.4 1.0 copy-done.2
  5.4 101.6 %layer.1 = (bf16[3,128,1280]{2,1,0:T(8,128)(2,1)S(1)}, f32[160,1280]{1,0:T(8,128)S(1)}) custom-call(s32[1]{0:T(128)S(6)} %copy.8.vc_ref, bf16[3,128,1280]{2,1,0:T(8,128)(2,1)S(1)} %copy-done.1, bf16[128,1280]{1,0:T(8,128)(2,1)S(1)} %copy-done.2, bf16[1280,1280]{1,0:T(8,128)(2,1)S(1)} %copy-done), custom_call_target="tpu_custom_call" | custom-call | tf_op jit(solution)/shard_map/layer/pallas_call | solution.py:469
  107.0 0.9 copy.9
  108.0 0.9 copy.10
Async XLA Ops:
  1.3 1.9 %copy-start = (bf16[1280,1280]{1,0:T(8,128)(2,1)S(1)}, bf16[1280,1280]{1,0:T(8,128)(2,1)}, u32[]{:S(2)}) copy-start(bf16[1280,1280]{1,0:T(8,128)(2,1)} %w_ref.1) | copy-start | bytes 9830404
  3.2 1.2 %copy-start.1 = (bf16[3,128,1280]{2,1,0:T(8,128)(2,1)S(1)}, bf16[3,128,1280]{2,1,0:T(8,128)(2,1)}, u32[]{:S(2)}) copy-start(bf16[3,128,1280]{2,1,0:T(8,128)(2,1)} %qkv_ref.1) | copy-start | bytes 2949124
  4.4 1.0 copy-start.2

commit v4 on v3

--- a/solution.py
+++ b/solution.py
@@ -36,10 +36,11 @@
 
 
 def kernel(
-    vc_ref, qkv_ref, cot_ref, w_ref, d_ref, wg_ref,
+    vc_ref, qkv_hbm, cot_hbm, w_ref, d_ref, wg_ref,
+    qkv_ref, cot_ref, rel,
     wv, wc, qs, qr, cs, cr, cx, xs, xr, cg, hq, hk, hv, hg, pf, pr, dt, da, db, dc, ra, rb, rc, ot,
     ws, wr, wown, x_s, x_r, zown, zs, zr, yb, yr, fc,
-    wsem, q_ss, q_rs, c_ss, c_rs, x_ss, x_rs, da_ss, da_rs, db_ss, db_rs, dc_ss, dc_rs, own_s, k_ss, k_rs, xx_ss, xx_rs,
+    wsem, q_ss, q_rs, c_lo, c_hi, c_out, c_rs, rel_rs, x_ss, x_rs, da_ss, da_rs, db_ss, db_rs, dc_ss, dc_rs, own_s, k_ss, k_rs, xx_ss, xx_rs,
     z_ss, z_rs, y_ss, y_rs, za_ss, za_rs, xa_ss, xa_rs, ka_ss, ka_rs,
 ):
     scene = lax.axis_index("scene")
@@ -84,6 +85,10 @@
         w_ref.at[pl.ds(pl.multiple_of(group * GW, GW), GW)], wv, wsem.at[0]
     )
     w_cross = pltpu.make_async_copy(w_ref.at[pl.ds(VIEW_W, CROSS_W)], wc, wsem.at[1])
+    for k in range(3):
+        pltpu.make_async_copy(qkv_hbm.at[k], qkv_ref.at[k], wsem.at[2 + k]).start()
+    cot_in = pltpu.make_async_copy(cot_hbm, cot_ref, wsem.at[5])
+    cot_in.start()
     w_cross.start()
     w_view.start()
 
@@ -93,6 +98,8 @@
 
     row = lax.broadcasted_iota(jnp.int32, (POS, 2 * POS), 0)
     col = lax.broadcasted_iota(jnp.int32, (POS, 2 * POS), 1)
+    for k in range(3):
+        pltpu.make_async_copy(qkv_hbm.at[k], qkv_ref.at[k], wsem.at[2 + k]).wait()
     for v in range(2):
         pick = jnp.where(col == 2 * row + v, 1.0, 0.0).astype(BF16)
         parts = []
@@ -117,12 +124,108 @@
         at = y if mine else p
         return remote(qs.at[p], rows_of(qr, at), q_ss.at[d], q_rs.at[at], to_y(p))
 
-    def c_copy(d, mine):
-        p = y_at(d)
-        at = y if mine else p
-        return remote(
-            cs.at[lax.div(p, GROUPS)], rows_of(cr, at), c_ss.at[d], c_rs.at[at], to_y(p)
-        )
+    place_in = lax.rem(y, GROUPS)
+    down, up = to_y(y_at(NY - 1)), to_y(y_at(1))
+
+    def half_of(ref, p, h):
+        return ref.at[pl.ds(pl.multiple_of(p * POS, POS), POS), pl.ds(h * HALF, HALF)]
+
+    def sorted_rows(v, h):
+        return cs.at[v, :, pl.ds(h * HALF, HALF)]
+
+    def go_down(k, h):
+        s = y_at(k)
+        src = sorted_rows(view, h) if k == 0 else half_of(cr, s, h)
+        return remote(src, half_of(cr, s, h), c_lo.at[h, k], c_rs.at[h, s], down)
+
+    def go_up(k, h):
+        s = y_at(NY - k)
+        src = sorted_rows(view, h) if k == 0 else half_of(cr, s, h)
+        return remote(src, half_of(cr, s, h), c_hi.at[h, k], c_rs.at[h, s], up)
+
+    def arrives(s, h):
+        return remote(half_of(cr, s, h), half_of(cr, s, h), c_lo.at[h, 0], c_rs.at[h, s], up)
+
+    def enter(n, h):
+        mine, relayed = sorted_rows(1 - view, h), rel.at[h]
+        if n == 0:
+            return remote(mine, half_of(cr, y, h), c_out.at[h, 0], c_rs.at[h, y], down)
+        if n == 1:
+            return remote(mine, relayed, c_out.at[h, 0], rel_rs.at[h], down)
+        if n == 2:
+            return remote(mine, relayed, c_out.at[h, 0], rel_rs.at[h], up)
+        return remote(mine, half_of(cr, y, h), c_out.at[h, 0], c_rs.at[h, y], up)
+
+    def relay(n, h):
+        s, to = (y_at(1), down) if n == 0 else (y_at(NY - 1), up)
+        return remote(rel.at[h], half_of(cr, s, h), c_out.at[h, 1], c_rs.at[h, s], to)
+
+    def relay_in(h):
+        return remote(rel.at[h], rel.at[h], c_out.at[h, 1], rel_rs.at[h], up)
+
+    def cot_start(h):
+        @pl.when(place_in >= 1)
+        def _():
+            go_down(0, h).start()
+
+        @pl.when(place_in <= 2)
+        def _():
+            go_up(0, h).start()
+
+        for n in range(GROUPS):
+
+            @pl.when(place_in == n)
+            def _():
+                enter(n, h).start()
+
+    def cot_flow(h):
+        for n in (0, 3):
+
+            @pl.when(place_in == n)
+            def _():
+                relay_in(h).wait_recv()
+                relay(n, h).start()
+
+        for k in range(1, 6):
+
+            @pl.when(place_in <= 5 - k)
+            def _():
+                arrives(y_at(k), h).wait_recv()
+
+                @pl.when(place_in >= 1)
+                def _():
+                    go_down(k, h).start()
+
+            @pl.when(place_in >= k - 2)
+            def _():
+                arrives(y_at(NY - k), h).wait_recv()
+
+                @pl.when(place_in <= 2)
+                def _():
+                    go_up(k, h).start()
+
+    def cot_end(h):
+        for n in range(GROUPS):
+
+            @pl.when(place_in == n)
+            def _():
+                enter(n, h).wait_send()
+
+        for n in (0, 3):
+
+            @pl.when(place_in == n)
+            def _():
+                relay(n, h).wait_send()
+
+        for k in range(6):
+
+            @pl.when(jnp.logical_and(place_in <= 5 - k, place_in >= 1))
+            def _():
+                go_down(k, h).wait_send()
+
+            @pl.when(jnp.logical_and(place_in >= k - 2, place_in <= 2))
+            def _():
+                go_up(k, h).wait_send()
 
     def x_copy(d, mine):
         p = y_at(d)
@@ -149,11 +252,12 @@
     for d in range(1, NY):
         q_copy(d, True).start()
     q_own.start()
+    cot_in.wait()
     for v in range(2):
         pick = jnp.where(col == 2 * row + v, 1.0, 0.0).astype(BF16)
         cs[v] = dot(pick, cot_ref[...]).astype(BF16)
-    for d in range(1, NY):
-        c_copy(d, True).start()
+    for h in range(2):
+        cot_start(h)
     c_own.start()
 
     w_cross.wait()
@@ -245,8 +349,8 @@
         grads = dt[...]
         return dot(k, grads, TN).T, dot(grads, hq[h]), dot(pr[h], hg[h])
 
-    for d in range(1, NY):
-        c_copy(d, False).wait_recv()
+    for h in range(2):
+        cot_flow(h)
     c_own.wait()
     for d in range(1, NY):
         x_copy(d, False).wait_recv()
@@ -432,9 +536,10 @@
                 at = 32 * i + 8 * xx
                 wg_ref[at : at + 8, cc * HALF : (cc + 1) * HALF] = fc[cc, xx, i].astype(F32)
 
+    for h in range(2):
+        cot_end(h)
     for d in range(1, NY):
         q_copy(d, True).wait_send()
-        c_copy(d, True).wait_send()
         x_copy(d, True).wait_send()
         for n in range(3):
             d_copy(n, d, True).wait_send()
@@ -464,6 +569,7 @@
 
 def on_device(qkv, view_counts, out_weight, out_cotangent):
     vmem = pl.BlockSpec(memory_space=pltpu.VMEM)
+    hbm = pl.BlockSpec(memory_space=pltpu.HBM)
     V = pltpu.VMEM
     S = pltpu.SemaphoreType.DMA
     return pl.pallas_call(
@@ -473,10 +579,11 @@
             jax.ShapeDtypeStruct((WIDTH // NY, WIDTH), F32),
         ),
         in_specs=[
-            pl.BlockSpec(memory_space=pltpu.SMEM), vmem, vmem, pl.BlockSpec(memory_space=pltpu.HBM),
+            pl.BlockSpec(memory_space=pltpu.SMEM), hbm, hbm, hbm,
         ],
         out_specs=(vmem, vmem),
         scratch_shapes=[
+            V((3, 2 * POS, WIDTH), BF16), V((2 * POS, WIDTH), BF16), V((2, POS, HALF), BF16),
             V((GW, WIDTH), BF16), V((CROSS_W, WIDTH), BF16),
             V((NY, POS, PACK), BF16), V((TV, PACK), BF16),
             V((2, POS, WIDTH), BF16), V((TV, WIDTH), BF16),
@@ -493,7 +600,9 @@
             V((NX, BLOCKS * 8, HALF), BF16), V((NX, BLOCKS * 8, HALF), BF16),
             V((NZ, 8, HALF), F32), V((NZ, 8, HALF), BF16), V((NZ, 8, HALF), BF16),
             V((8, HALF), BF16), V((2, 8, HALF), BF16), V((2, NX, OWNED, 8, HALF), BF16),
-            S((2,)), S((NY,)), S((NY,)), S((NY,)), S((NY,)), S((NY,)), S((NY,)),
+            S((6,)), S((NY,)), S((NY,)),
+            S((2, 6)), S((2, 6)), S((2, 2)), S((2, NY)), S((2,)),
+            S((NY,)), S((NY,)),
             S((NY,)), S((NY,)), S((NY,)), S((NY,)), S((NY,)), S((NY,)), S((8,)), S, S, S((NX,)), S((NX,)),
             S((NZ,)), S((NZ,)), S, S((2,)), S((NZ,)), S((OWNED,)), S((NX,)), S((NX,)), S, S,
         ],
@@ -501,7 +610,7 @@
             collective_id=0, has_side_effects=True, vmem_limit_bytes=30 * 1024 * 1024
         ),
         name="layer",
-    )(view_counts, qkv, out_cotangent, out_weight)
+    )(view_counts, *(pltpu.with_memory_space_constraint(a, pltpu.HBM) for a in (qkv, out_cotangent, out_weight)))
 
 
 def solution(mesh):

time: 109 us -> 109 us (level)
  local copies, waits for them, and re-layouts: 5.93 us -> 1.84 us
  Pallas kernels: 102 us -> 106 us
    pallas_call x1, Pallas kernels: 102 us -> 106 us  [on_device(): pl.pallas_call(kernel, out_shape=(jax.ShapeDtypeStruct((3, 2 * POS, WIDTH...]
    unnamed x8 -> x2, local copies, waits for them, and re-layouts: 5.93 us -> 1.84 us
where the time goes in v4:
time: 109 us
  Pallas kernels  106 us (97%)
  local copies, waits for them, and re-layouts  1.84 us (2%)
  between operations  1.28 us (1%)
    pallas_call x1, Pallas kernels, on_device(): pl.pallas_call(kernel, out_shape=(jax.ShapeDtypeStruct((3, 2 * POS, WIDTH...  106 us

profile of v4, /device:TPU:1, one launch (start us, length us, event | category | flops | bytes accessed | tf_op | source)
XLA Modules:
  0.0 109.2 jit_solution(15989681352761980556)
XLA Ops:
  1.3 106.1 %layer.1 = (bf16[3,128,1280]{2,1,0:T(8,128)(2,1)S(1)}, f32[160,1280]{1,0:T(8,128)S(1)}) custom-call(s32[1]{0:T(128)S(6)} %copy.8.vc_ref, bf16[3,128,1280]{2,1,0:T(8,128)(2,1)} %qkv_hbm.1, bf16[128,1280]{1,0:T(8,128)(2,1)} %cot_hbm.1, bf16[1280,1280]{1,0:T(8,128)(2,1)} %w_ref.1), custom_call_target="tpu_custom_call" | custom-call | tf_op jit(solution)/shard_map/layer/pallas_call | solution.py:575
  107.4 0.9 copy.9
  108.3 0.9 copy.10

commit v5 on v4

--- a/solution.py
+++ b/solution.py
@@ -96,6 +96,15 @@
     live = [jnp.where(vc > v, 1.0, 0.0).astype(F32) for v in range(2)]
     my_live = jnp.where(vc > view, 1.0, 0.0).astype(F32)
 
+    def rows_of(ref, p):
+        return ref.at[pl.ds(pl.multiple_of(p * POS, POS), POS)]
+
+    def q_send(p):
+        return remote(qs.at[p], rows_of(qr, y), q_ss.at[p], q_rs.at[y], to_y(p))
+
+    def q_arrives(p):
+        return remote(rows_of(qr, p), rows_of(qr, p), q_ss.at[0], q_rs.at[p], to_y(p))
+
     row = lax.broadcasted_iota(jnp.int32, (POS, 2 * POS), 0)
     col = lax.broadcasted_iota(jnp.int32, (POS, 2 * POS), 1)
     for k in range(3):
@@ -104,25 +113,21 @@
         pick = jnp.where(col == 2 * row + v, 1.0, 0.0).astype(BF16)
         parts = []
         for k in range(3):
-            r = dot(pick, qkv_ref[k])
-            cx[k, v] = r[:, VIEW_W:]
-            parts.append(r[:, :VIEW_W])
+            parts.append(dot(pick, qkv_ref[k, :, :VIEW_W]))
         for g in range(GROUPS):
             cols = slice(g * GW, (g + 1) * GW)
             packed = jnp.concatenate(
                 [p[:, cols] for p in parts] + [jnp.zeros((POS, PACK - 3 * GW), F32)], axis=1
             )
             qs[v * GROUPS + g] = packed.astype(BF16)
-
-    pl.semaphore_wait(barrier, len(peers))
-
-    def rows_of(ref, p):
-        return ref.at[pl.ds(pl.multiple_of(p * POS, POS), POS)]
-
-    def q_copy(d, mine):
-        p = y_at(d)
-        at = y if mine else p
-        return remote(qs.at[p], rows_of(qr, at), q_ss.at[d], q_rs.at[at], to_y(p))
+        if v == 0:
+            pl.semaphore_wait(barrier, len(peers))
+        for p in range(v * GROUPS, (v + 1) * GROUPS):
+
+            @pl.when(p != y)
+            def _():
+                q_send(p).start()
+
 
     place_in = lax.rem(y, GROUPS)
     down, up = to_y(y_at(NY - 1)), to_y(y_at(1))
@@ -178,31 +183,33 @@
             def _():
                 enter(n, h).start()
 
-    def cot_flow(h):
+    def cot_flow():
         for n in (0, 3):
 
             @pl.when(place_in == n)
             def _():
-                relay_in(h).wait_recv()
-                relay(n, h).start()
+                for h in range(2):
+                    relay_in(h).wait_recv()
+                    relay(n, h).start()
 
         for k in range(1, 6):
-
-            @pl.when(place_in <= 5 - k)
-            def _():
-                arrives(y_at(k), h).wait_recv()
-
-                @pl.when(place_in >= 1)
+            for h in range(2):
+
+                @pl.when(place_in <= 5 - k)
                 def _():
-                    go_down(k, h).start()
-
-            @pl.when(place_in >= k - 2)
-            def _():
-                arrives(y_at(NY - k), h).wait_recv()
-
-                @pl.when(place_in <= 2)
+                    arrives(y_at(k), h).wait_recv()
+
+                    @pl.when(place_in >= 1)
+                    def _():
+                        go_down(k, h).start()
+
+                @pl.when(place_in >= k - 2)
                 def _():
-                    go_up(k, h).start()
+                    arrives(y_at(NY - k), h).wait_recv()
+
+                    @pl.when(place_in <= 2)
+                    def _():
+                        go_up(k, h).start()
 
     def cot_end(h):
         for n in range(GROUPS):
@@ -249,8 +256,6 @@
     c_own = pltpu.make_async_copy(cs.at[view], rows_of(cr, y), own_s.at[1])
     x_own = pltpu.make_async_copy(xs.at[y], rows_of(xr, y), own_s.at[2])
 
-    for d in range(1, NY):
-        q_copy(d, True).start()
     q_own.start()
     cot_in.wait()
     for v in range(2):
@@ -259,6 +264,10 @@
     for h in range(2):
         cot_start(h)
     c_own.start()
+    for v in range(2):
+        pick = jnp.where(col == 2 * row + v, 1.0, 0.0).astype(BF16)
+        for k in range(3):
+            cx[k, v] = dot(pick, qkv_ref[k, :, VIEW_W:])
 
     w_cross.wait()
     same = jnp.where(
@@ -313,7 +322,7 @@
         cg[2, v] = dv[v].astype(BF16)
 
     for d in range(1, NY):
-        q_copy(d, False).wait_recv()
+        q_arrives(y_at(d)).wait_recv()
     q_own.wait()
     packed = qr[...]
     for h in range(HEADS):
@@ -349,8 +358,7 @@
         grads = dt[...]
         return dot(k, grads, TN).T, dot(grads, hq[h]), dot(pr[h], hg[h])
 
-    for h in range(2):
-        cot_flow(h)
+    cot_flow()
     c_own.wait()
     for d in range(1, NY):
         x_copy(d, False).wait_recv()
@@ -421,10 +429,6 @@
 
     dq2, dk2, dv2 = backward(2)
     dc[...] = jnp.concatenate([dq2, dk2, dv2, jnp.zeros((TV, HD), F32)], axis=1).astype(BF16)
-    for d in range(1, NY):
-        d_copy(2, d, True).start()
-    d_own[2].start()
-
     late = lax.div(z, 6)
     mine_at = local_block(z)
     blk = (1 - late) * (6 * group + mine_at) + late * (18 + 4 * group + mine_at)
@@ -449,6 +453,10 @@
     @pl.when(here)
     def _():
         y_own.start()
+
+    for d in range(1, NY):
+        d_copy(2, d, True).start()
+    d_own[2].start()
 
     tokens = TV * 2 * NZ * NX * 2
     slots = []
@@ -523,23 +531,32 @@
         piece = fc.at[c, x if mine else p]
         return remote(piece, piece, xa_ss.at[d], xa_rs.at[x if mine else p], to_scene(z, p, c))
 
+    def ka_copy(cc, xx):
+        return remote(fc.at[cc, xx], fc.at[cc, xx], ka_ss.at[xx], ka_rs.at[xx], core_peer)
+
     for d in range(1, NX):
         xa_copy(d, True).start()
-    for d in range(1, NX):
+    ka_copy(c, x).start()
+    for d in (1, 3, 2):
         xa_copy(d, False).wait_recv()
-    ka_copy = remote(fc.at[c], fc.at[c], ka_ss, ka_rs, core_peer)
-    ka_copy.start()
-    remote(fc.at[1 - c], fc.at[1 - c], ka_ss, ka_rs, core_peer).wait_recv()
+        ka_copy(c, x_at(d)).start()
+    for xx in range(NX):
+        ka_copy(1 - c, xx).wait_recv()
     for cc in range(2):
         for xx in range(NX):
             for i in range(OWNED):
                 at = 32 * i + 8 * xx
                 wg_ref[at : at + 8, cc * HALF : (cc + 1) * HALF] = fc[cc, xx, i].astype(F32)
 
+    for p in range(NY):
+
+        @pl.when(p != y)
+        def _():
+            q_send(p).wait_send()
+
     for h in range(2):
         cot_end(h)
     for d in range(1, NY):
-        q_copy(d, True).wait_send()
         x_copy(d, True).wait_send()
         for n in range(3):
             d_copy(n, d, True).wait_send()
@@ -564,7 +581,8 @@
             for d in range(1, NZ):
                 za_copy(i, d).wait_send()
 
-    ka_copy.wait_send()
+    for xx in range(NX):
+        ka_copy(c, xx).wait_send()
 
 
 def on_device(qkv, view_counts, out_weight, out_cotangent):
@@ -604,7 +622,7 @@
             S((2, 6)), S((2, 6)), S((2, 2)), S((2, NY)), S((2,)),
             S((NY,)), S((NY,)),
             S((NY,)), S((NY,)), S((NY,)), S((NY,)), S((NY,)), S((NY,)), S((8,)), S, S, S((NX,)), S((NX,)),
-            S((NZ,)), S((NZ,)), S, S((2,)), S((NZ,)), S((OWNED,)), S((NX,)), S((NX,)), S, S,
+            S((NZ,)), S((NZ,)), S, S((2,)), S((NZ,)), S((OWNED,)), S((NX,)), S((NX,)), S((NX,)), S((NX,)),
         ],
         compiler_params=pltpu.CompilerParams(
             collective_id=0, has_side_effects=True, vmem_limit_bytes=30 * 1024 * 1024

time: 109 us -> 97.5 us (0.89)
  Pallas kernels: 106 us -> 94.2 us
    pallas_call x1, Pallas kernels: 106 us -> 94.2 us  [on_device(): pl.pallas_call(kernel, out_shape=(jax.ShapeDtypeStruct((3, 2 * POS, WIDTH...]
where the time goes in v5:
time: 97.5 us; the launch traced here: 97.3 us
  Pallas kernels  94.2 us (97%)
  local copies, waits for them, and re-layouts  1.84 us (2%)
  between operations  1.28 us (1%)
    pallas_call x1, Pallas kernels, on_device(): pl.pallas_call(kernel, out_shape=(jax.ShapeDtypeStruct((3, 2 * POS, WIDTH...  94.2 us

profile of v5, /device:TPU:1, one launch (start us, length us, event | category | flops | bytes accessed | tf_op | source)
XLA Modules:
  0.0 97.3 jit_solution(9893476050162754743)
XLA Ops:
  1.3 94.2 %layer.1 = (bf16[3,128,1280]{2,1,0:T(8,128)(2,1)S(1)}, f32[160,1280]{1,0:T(8,128)S(1)}) custom-call(s32[1]{0:T(128)S(6)} %copy.8.vc_ref, bf16[3,128,1280]{2,1,0:T(8,128)(2,1)} %qkv_hbm.1, bf16[128,1280]{1,0:T(8,128)(2,1)} %cot_hbm.1, bf16[1280,1280]{1,0:T(8,128)(2,1)} %w_ref.1), custom_call_target="tpu_custom_call" | custom-call | tf_op jit(solution)/shard_map/layer/pallas_call | solution.py:593
  95.5 0.9 copy.9
  96.4 0.9 copy.10

commit v6 on v5

--- a/solution.py
+++ b/solution.py
@@ -25,7 +25,6 @@
 CROSS_W = 512
 WIDTH = 1280
 GW = HEADS * HD
-PACK = 640
 HALF = WIDTH // 2
 BLOCKS = 10
 OWNED = 5
@@ -38,9 +37,9 @@
 def kernel(
     vc_ref, qkv_hbm, cot_hbm, w_ref, d_ref, wg_ref,
     qkv_ref, cot_ref, rel,
-    wv, wc, qs, qr, cs, cr, cx, xs, xr, cg, hq, hk, hv, hg, pf, pr, dt, da, db, dc, ra, rb, rc, ot,
+    wv, wc, qs, qr, qe, qx, cs, cr, cx, xs, xr, cg, hq, hk, hv, hg, pf, pr, dt, da, db, dc, ra, rb, rc, ot,
     ws, wr, wown, x_s, x_r, zown, zs, zr, yb, yr, fc,
-    wsem, q_ss, q_rs, c_lo, c_hi, c_out, c_rs, rel_rs, x_ss, x_rs, da_ss, da_rs, db_ss, db_rs, dc_ss, dc_rs, own_s, k_ss, k_rs, xx_ss, xx_rs,
+    wsem, q_ss, q_rs, e_ss, e_rs, c_lo, c_hi, c_out, c_rs, rel_rs, x_ss, x_rs, da_ss, da_rs, db_ss, db_rs, dc_ss, dc_rs, own_s, k_ss, k_rs, xx_ss, xx_rs,
     z_ss, z_rs, y_ss, y_rs, za_ss, za_rs, xa_ss, xa_rs, ka_ss, ka_rs,
 ):
     scene = lax.axis_index("scene")
@@ -99,11 +98,19 @@
     def rows_of(ref, p):
         return ref.at[pl.ds(pl.multiple_of(p * POS, POS), POS)]
 
+    def extra_of(ref, p):
+        return ref.at[pl.ds(pl.multiple_of(p * (POS // 2), POS // 2), POS // 2)]
+
     def q_send(p):
-        return remote(qs.at[p], rows_of(qr, y), q_ss.at[p], q_rs.at[y], to_y(p))
+        return (
+            remote(qs.at[p], rows_of(qr, y), q_ss.at[p], q_rs.at[y], to_y(p)),
+            remote(qe.at[p], extra_of(qx, y), e_ss.at[p], e_rs.at[y], to_y(p)),
+        )
 
     def q_arrives(p):
-        return remote(rows_of(qr, p), rows_of(qr, p), q_ss.at[0], q_rs.at[p], to_y(p))
+        main, extra = rows_of(qr, p), extra_of(qx, p)
+        remote(main, main, q_ss.at[0], q_rs.at[p], to_y(p)).wait_recv()
+        remote(extra, extra, e_ss.at[0], e_rs.at[p], to_y(p)).wait_recv()
 
     row = lax.broadcasted_iota(jnp.int32, (POS, 2 * POS), 0)
     col = lax.broadcasted_iota(jnp.int32, (POS, 2 * POS), 1)
@@ -116,17 +123,23 @@
             parts.append(dot(pick, qkv_ref[k, :, :VIEW_W]))
         for g in range(GROUPS):
             cols = slice(g * GW, (g + 1) * GW)
+            last = parts[2][:, cols]
             packed = jnp.concatenate(
-                [p[:, cols] for p in parts] + [jnp.zeros((POS, PACK - 3 * GW), F32)], axis=1
+                [parts[0][:, cols], parts[1][:, cols], last[:, : 2 * HD]], axis=1
             )
             qs[v * GROUPS + g] = packed.astype(BF16)
+            tail = last[:, 2 * HD :]
+            qe[v * GROUPS + g] = jnp.concatenate(
+                [tail[: POS // 2], tail[POS // 2 :]], axis=1
+            ).astype(BF16)
         if v == 0:
             pl.semaphore_wait(barrier, len(peers))
         for p in range(v * GROUPS, (v + 1) * GROUPS):
 
             @pl.when(p != y)
             def _():
-                q_send(p).start()
+                for part in q_send(p):
+                    part.start()
 
 
     place_in = lax.rem(y, GROUPS)
@@ -183,7 +196,7 @@
             def _():
                 enter(n, h).start()
 
-    def cot_flow():
+    def cot_relay():
         for n in (0, 3):
 
             @pl.when(place_in == n)
@@ -192,7 +205,8 @@
                     relay_in(h).wait_recv()
                     relay(n, h).start()
 
-        for k in range(1, 6):
+    def cot_flow(hops):
+        for k in hops:
             for h in range(2):
 
                 @pl.when(place_in <= 5 - k)
@@ -253,10 +267,12 @@
     ]
 
     q_own = pltpu.make_async_copy(qs.at[y], rows_of(qr, y), own_s.at[0])
+    e_own = pltpu.make_async_copy(qe.at[y], extra_of(qx, y), own_s.at[3])
     c_own = pltpu.make_async_copy(cs.at[view], rows_of(cr, y), own_s.at[1])
     x_own = pltpu.make_async_copy(xs.at[y], rows_of(xr, y), own_s.at[2])
 
     q_own.start()
+    e_own.start()
     cot_in.wait()
     for v in range(2):
         pick = jnp.where(col == 2 * row + v, 1.0, 0.0).astype(BF16)
@@ -322,13 +338,17 @@
         cg[2, v] = dv[v].astype(BF16)
 
     for d in range(1, NY):
-        q_arrives(y_at(d)).wait_recv()
+        q_arrives(y_at(d))
     q_own.wait()
+    e_own.wait()
     packed = qr[...]
     for h in range(HEADS):
         hq[h] = packed[:, h * HD : (h + 1) * HD]
         hk[h] = packed[:, GW + h * HD : GW + (h + 1) * HD]
-        hv[h] = packed[:, 2 * GW + h * HD : 2 * GW + (h + 1) * HD]
+        if h < 2:
+            hv[h] = packed[:, 2 * GW + h * HD : 2 * GW + (h + 1) * HD]
+    extra = qx[...].reshape(NY, POS // 2, 2 * HD)
+    hv[2] = jnp.concatenate([extra[:, :, :HD], extra[:, :, HD:]], axis=1).reshape(TV, HD)
     chunk = 128
 
     def forward(h, carry):
@@ -358,23 +378,36 @@
         grads = dt[...]
         return dot(k, grads, TN).T, dot(grads, hq[h]), dot(pr[h], hg[h])
 
-    cot_flow()
-    c_own.wait()
+    cot_relay()
+    cot_flow((1, 2, 3))
     for d in range(1, NY):
         x_copy(d, False).wait_recv()
     x_own.wait()
+    ot[GW:, :] = xr[...].astype(F32).T.astype(BF16)
+    cot_flow((4, 5))
+    c_own.wait()
 
     def partial(cc):
         cols = pl.ds(pl.multiple_of(cc * HALF, HALF), HALF)
-        return jnp.concatenate(
-            [dot(ot[...], cr[:, cols]), dot(xr[...], cr[:, cols], TN)], axis=0
-        )
+        return dot(ot[...], cr[:, cols])
 
     ws[...] = partial(1 - c).astype(BF16)
     k_copy = remote(ws, wr, k_ss, k_rs, core_peer)
     k_copy.start()
     wown[...] = partial(c).reshape(BLOCKS, NX, 8, HALF)
 
+    k_copy.wait_recv()
+    wown[...] = wown[...] + wr[...].astype(F32).reshape(BLOCKS, NX, 8, HALF)
+    for i in range(NX):
+        x_s[i] = wown[:, i].reshape(BLOCKS * 8, HALF).astype(BF16)
+
+    def xx_copy(d, mine):
+        p = x_at(d)
+        at = x if mine else p
+        return remote(x_s.at[p], x_r.at[at], xx_ss.at[d], xx_rs.at[at], to_scene(z, p, c))
+
+    for d in range(1, NX):
+        xx_copy(d, True).start()
     w_view.wait()
     g_all = (dot(cr[...], wv[...], NT).astype(BF16).astype(F32) * my_live).astype(BF16)
     for h in range(HEADS):
@@ -386,18 +419,6 @@
         d_copy(0, d, True).start()
     d_own[0].start()
 
-    k_copy.wait_recv()
-    wown[...] = wown[...] + wr[...].astype(F32).reshape(BLOCKS, NX, 8, HALF)
-    for i in range(NX):
-        x_s[i] = wown[:, i].reshape(BLOCKS * 8, HALF).astype(BF16)
-
-    def xx_copy(d, mine):
-        p = x_at(d)
-        at = x if mine else p
-        return remote(x_s.at[p], x_r.at[at], xx_ss.at[d], xx_rs.at[at], to_scene(z, p, c))
-
-    for d in range(1, NX):
-        xx_copy(d, True).start()
     dq1, dk1, dv1 = backward(1)
     db[:, : 2 * HD] = jnp.concatenate([dq1, dk1], axis=1).astype(BF16)
     db[:, 3 * HD :] = dv1.astype(BF16)
@@ -552,7 +573,8 @@
 
         @pl.when(p != y)
         def _():
-            q_send(p).wait_send()
+            for part in q_send(p):
+                part.wait_send()
 
     for h in range(2):
         cot_end(h)
@@ -603,7 +625,8 @@
         scratch_shapes=[
             V((3, 2 * POS, WIDTH), BF16), V((2 * POS, WIDTH), BF16), V((2, POS, HALF), BF16),
             V((GW, WIDTH), BF16), V((CROSS_W, WIDTH), BF16),
-            V((NY, POS, PACK), BF16), V((TV, PACK), BF16),
+            V((NY, POS, 512), BF16), V((TV, 512), BF16),
+            V((NY, POS // 2, 128), BF16), V((TV // 2, 128), BF16),
             V((2, POS, WIDTH), BF16), V((TV, WIDTH), BF16),
             V((3, 2, POS, CROSS_W), F32),
             V((NY, POS, 128), BF16), V((TV, 128), BF16),
@@ -613,12 +636,12 @@
             V((HEADS, TV, TV), F32), V((HEADS, TV, TV), BF16), V((TV, TV), BF16),
             V((TV, 128), BF16), V((TV, 256), BF16), V((TV, 256), BF16),
             V((NY, POS, 128), BF16), V((NY, POS, 256), BF16), V((NY, POS, 256), BF16),
-            V((GW, TV), BF16),
+            V((320, TV), BF16),
             V((320, HALF), BF16), V((320, HALF), BF16), V((BLOCKS, NX, 8, HALF), F32),
             V((NX, BLOCKS * 8, HALF), BF16), V((NX, BLOCKS * 8, HALF), BF16),
             V((NZ, 8, HALF), F32), V((NZ, 8, HALF), BF16), V((NZ, 8, HALF), BF16),
             V((8, HALF), BF16), V((2, 8, HALF), BF16), V((2, NX, OWNED, 8, HALF), BF16),
-            S((6,)), S((NY,)), S((NY,)),
+            S((6,)), S((NY,)), S((NY,)), S((NY,)), S((NY,)),
             S((2, 6)), S((2, 6)), S((2, 2)), S((2, NY)), S((2,)),
             S((NY,)), S((NY,)),
             S((NY,)), S((NY,)), S((NY,)), S((NY,)), S((NY,)), S((NY,)), S((8,)), S, S, S((NX,)), S((NX,)),

time: 97.5 us -> 95.7 us (0.982)
  Pallas kernels: 94.2 us -> 92.4 us
    pallas_call x1, Pallas kernels: 94.2 us -> 92.4 us  [on_device(): pl.pallas_call(kernel, out_shape=(jax.ShapeDtypeStruct((3, 2 * POS, WIDTH...]
where the time goes in v6:
time: 95.7 us; the launch traced here: 95.5 us
  Pallas kernels  92.4 us (97%)
  local copies, waits for them, and re-layouts  1.84 us (2%)
  between operations  1.28 us (1%)
    pallas_call x1, Pallas kernels, on_device(): pl.pallas_call(kernel, out_shape=(jax.ShapeDtypeStruct((3, 2 * POS, WIDTH...  92.4 us

profile of v6, /device:TPU:1, one launch (start us, length us, event | category | flops | bytes accessed | tf_op | source)
XLA Modules:
  0.0 95.5 jit_solution(5834339395008958651)
XLA Ops:
  1.3 92.4 %layer.1 = (bf16[3,128,1280]{2,1,0:T(8,128)(2,1)S(1)}, f32[160,1280]{1,0:T(8,128)S(1)}) custom-call(s32[1]{0:T(128)S(6)} %copy.8.vc_ref, bf16[3,128,1280]{2,1,0:T(8,128)(2,1)} %qkv_hbm.1, bf16[128,1280]{1,0:T(8,128)(2,1)} %cot_hbm.1, bf16[1280,1280]{1,0:T(8,128)(2,1)} %w_ref.1), custom_call_target="tpu_custom_call" | custom-call | tf_op jit(solution)/shard_map/layer/pallas_call | solution.py:615
  93.7 0.9 copy.9
  94.6 0.9 copy.10

commit v7 on v6

--- a/solution.py
+++ b/solution.py
@@ -84,10 +84,10 @@
         w_ref.at[pl.ds(pl.multiple_of(group * GW, GW), GW)], wv, wsem.at[0]
     )
     w_cross = pltpu.make_async_copy(w_ref.at[pl.ds(VIEW_W, CROSS_W)], wc, wsem.at[1])
+    cot_in = pltpu.make_async_copy(cot_hbm, cot_ref, wsem.at[5])
+    cot_in.start()
     for k in range(3):
         pltpu.make_async_copy(qkv_hbm.at[k], qkv_ref.at[k], wsem.at[2 + k]).start()
-    cot_in = pltpu.make_async_copy(cot_hbm, cot_ref, wsem.at[5])
-    cot_in.start()
     w_cross.start()
     w_view.start()
 
@@ -114,6 +114,121 @@
 
     row = lax.broadcasted_iota(jnp.int32, (POS, 2 * POS), 0)
     col = lax.broadcasted_iota(jnp.int32, (POS, 2 * POS), 1)
+    place_in = lax.rem(y, GROUPS)
+    down, up = to_y(y_at(NY - 1)), to_y(y_at(1))
+
+    def half_of(ref, p, h):
+        return ref.at[pl.ds(pl.multiple_of(p * POS, POS), POS), pl.ds(h * HALF, HALF)]
+
+    def sorted_rows(v, h):
+        return cs.at[v, :, pl.ds(h * HALF, HALF)]
+
+    def go_down(k, h):
+        s = y_at(k)
+        src = sorted_rows(view, h) if k == 0 else half_of(cr, s, h)
+        return remote(src, half_of(cr, s, h), c_lo.at[h, k], c_rs.at[h, s], down)
+
+    def go_up(k, h):
+        s = y_at(NY - k)
+        src = sorted_rows(view, h) if k == 0 else half_of(cr, s, h)
+        return remote(src, half_of(cr, s, h), c_hi.at[h, k], c_rs.at[h, s], up)
+
+    def arrives(s, h):
+        return remote(half_of(cr, s, h), half_of(cr, s, h), c_lo.at[h, 0], c_rs.at[h, s], up)
+
+    def enter(n, h):
+        mine, relayed = sorted_rows(1 - view, h), rel.at[h]
+        if n == 0:
+            return remote(mine, half_of(cr, y, h), c_out.at[h, 0], c_rs.at[h, y], down)
+        if n == 1:
+            return remote(mine, relayed, c_out.at[h, 0], rel_rs.at[h], down)
+        if n == 2:
+            return remote(mine, relayed, c_out.at[h, 0], rel_rs.at[h], up)
+        return remote(mine, half_of(cr, y, h), c_out.at[h, 0], c_rs.at[h, y], up)
+
+    def relay(n, h):
+        s, to = (y_at(1), down) if n == 0 else (y_at(NY - 1), up)
+        return remote(rel.at[h], half_of(cr, s, h), c_out.at[h, 1], c_rs.at[h, s], to)
+
+    def relay_in(h):
+        return remote(rel.at[h], rel.at[h], c_out.at[h, 1], rel_rs.at[h], up)
+
+    def cot_start(h):
+        @pl.when(place_in >= 1)
+        def _():
+            go_down(0, h).start()
+
+        @pl.when(place_in <= 2)
+        def _():
+            go_up(0, h).start()
+
+        for n in range(GROUPS):
+
+            @pl.when(place_in == n)
+            def _():
+                enter(n, h).start()
+
+    def cot_relay():
+        for n in (0, 3):
+
+            @pl.when(place_in == n)
+            def _():
+                for h in range(2):
+                    relay_in(h).wait_recv()
+                    relay(n, h).start()
+
+    def cot_flow(hops):
+        for k in hops:
+            for h in range(2):
+
+                @pl.when(place_in <= 5 - k)
+                def _():
+                    arrives(y_at(k), h).wait_recv()
+
+                    @pl.when(place_in >= 1)
+                    def _():
+                        go_down(k, h).start()
+
+                @pl.when(place_in >= k - 2)
+                def _():
+                    arrives(y_at(NY - k), h).wait_recv()
+
+                    @pl.when(place_in <= 2)
+                    def _():
+                        go_up(k, h).start()
+
+    def cot_end(h):
+        for n in range(GROUPS):
+
+            @pl.when(place_in == n)
+            def _():
+                enter(n, h).wait_send()
+
+        for n in (0, 3):
+
+            @pl.when(place_in == n)
+            def _():
+                relay(n, h).wait_send()
+
+        for k in range(6):
+
+            @pl.when(jnp.logical_and(place_in <= 5 - k, place_in >= 1))
+            def _():
+                go_down(k, h).wait_send()
+
+            @pl.when(jnp.logical_and(place_in >= k - 2, place_in <= 2))
+            def _():
+                go_up(k, h).wait_send()
+
+    c_own = pltpu.make_async_copy(cs.at[view], rows_of(cr, y), own_s.at[1])
+    cot_in.wait()
+    for v in range(2):
+        pick = jnp.where(col == 2 * row + v, 1.0, 0.0).astype(BF16)
+        cs[v] = dot(pick, cot_ref[...]).astype(BF16)
+    pl.semaphore_wait(barrier, len(peers))
+    for h in range(2):
+        cot_start(h)
+    c_own.start()
     for k in range(3):
         pltpu.make_async_copy(qkv_hbm.at[k], qkv_ref.at[k], wsem.at[2 + k]).wait()
     for v in range(2):
@@ -132,8 +247,6 @@
             qe[v * GROUPS + g] = jnp.concatenate(
                 [tail[: POS // 2], tail[POS // 2 :]], axis=1
             ).astype(BF16)
-        if v == 0:
-            pl.semaphore_wait(barrier, len(peers))
         for p in range(v * GROUPS, (v + 1) * GROUPS):
 
             @pl.when(p != y)
@@ -141,112 +254,6 @@
                 for part in q_send(p):
                     part.start()
 
-
-    place_in = lax.rem(y, GROUPS)
-    down, up = to_y(y_at(NY - 1)), to_y(y_at(1))
-
-    def half_of(ref, p, h):
-        return ref.at[pl.ds(pl.multiple_of(p * POS, POS), POS), pl.ds(h * HALF, HALF)]
-
-    def sorted_rows(v, h):
-        return cs.at[v, :, pl.ds(h * HALF, HALF)]
-
-    def go_down(k, h):
-        s = y_at(k)
-        src = sorted_rows(view, h) if k == 0 else half_of(cr, s, h)
-        return remote(src, half_of(cr, s, h), c_lo.at[h, k], c_rs.at[h, s], down)
-
-    def go_up(k, h):
-        s = y_at(NY - k)
-        src = sorted_rows(view, h) if k == 0 else half_of(cr, s, h)
-        return remote(src, half_of(cr, s, h), c_hi.at[h, k], c_rs.at[h, s], up)
-
-    def arrives(s, h):
-        return remote(half_of(cr, s, h), half_of(cr, s, h), c_lo.at[h, 0], c_rs.at[h, s], up)
-
-    def enter(n, h):
-        mine, relayed = sorted_rows(1 - view, h), rel.at[h]
-        if n == 0:
-            return remote(mine, half_of(cr, y, h), c_out.at[h, 0], c_rs.at[h, y], down)
-        if n == 1:
-            return remote(mine, relayed, c_out.at[h, 0], rel_rs.at[h], down)
-        if n == 2:
-            return remote(mine, relayed, c_out.at[h, 0], rel_rs.at[h], up)
-        return remote(mine, half_of(cr, y, h), c_out.at[h, 0], c_rs.at[h, y], up)
-
-    def relay(n, h):
-        s, to = (y_at(1), down) if n == 0 else (y_at(NY - 1), up)
-        return remote(rel.at[h], half_of(cr, s, h), c_out.at[h, 1], c_rs.at[h, s], to)
-
-    def relay_in(h):
-        return remote(rel.at[h], rel.at[h], c_out.at[h, 1], rel_rs.at[h], up)
-
-    def cot_start(h):
-        @pl.when(place_in >= 1)
-        def _():
-            go_down(0, h).start()
-
-        @pl.when(place_in <= 2)
-        def _():
-            go_up(0, h).start()
-
-        for n in range(GROUPS):
-
-            @pl.when(place_in == n)
-            def _():
-                enter(n, h).start()
-
-    def cot_relay():
-        for n in (0, 3):
-
-            @pl.when(place_in == n)
-            def _():
-                for h in range(2):
-                    relay_in(h).wait_recv()
-                    relay(n, h).start()
-
-    def cot_flow(hops):
-        for k in hops:
-            for h in range(2):
-
-                @pl.when(place_in <= 5 - k)
-                def _():
-                    arrives(y_at(k), h).wait_recv()
-
-                    @pl.when(place_in >= 1)
-                    def _():
-                        go_down(k, h).start()
-
-                @pl.when(place_in >= k - 2)
-                def _():
-                    arrives(y_at(NY - k), h).wait_recv()
-
-                    @pl.when(place_in <= 2)
-                    def _():
-                        go_up(k, h).start()
-
-    def cot_end(h):
-        for n in range(GROUPS):
-
-            @pl.when(place_in == n)
-            def _():
-                enter(n, h).wait_send()
-
-        for n in (0, 3):
-
-            @pl.when(place_in == n)
-            def _():
-                relay(n, h).wait_send()
-
-        for k in range(6):
-
-            @pl.when(jnp.logical_and(place_in <= 5 - k, place_in >= 1))
-            def _():
-                go_down(k, h).wait_send()
-
-            @pl.when(jnp.logical_and(place_in >= k - 2, place_in <= 2))
-            def _():
-                go_up(k, h).wait_send()
 
     def x_copy(d, mine):
         p = y_at(d)
@@ -268,18 +275,10 @@
 
     q_own = pltpu.make_async_copy(qs.at[y], rows_of(qr, y), own_s.at[0])
     e_own = pltpu.make_async_copy(qe.at[y], extra_of(qx, y), own_s.at[3])
-    c_own = pltpu.make_async_copy(cs.at[view], rows_of(cr, y), own_s.at[1])
     x_own = pltpu.make_async_copy(xs.at[y], rows_of(xr, y), own_s.at[2])
 
     q_own.start()
     e_own.start()
-    cot_in.wait()
-    for v in range(2):
-        pick = jnp.where(col == 2 * row + v, 1.0, 0.0).astype(BF16)
-        cs[v] = dot(pick, cot_ref[...]).astype(BF16)
-    for h in range(2):
-        cot_start(h)
-    c_own.start()
     for v in range(2):
         pick = jnp.where(col == 2 * row + v, 1.0, 0.0).astype(BF16)
         for k in range(3):
@@ -337,6 +336,9 @@
         cg[1, v] = dk[v].astype(BF16)
         cg[2, v] = dv[v].astype(BF16)
 
+    cot_relay()
+    cot_flow((1, 2))
+
     for d in range(1, NY):
         q_arrives(y_at(d))
     q_own.wait()
@@ -378,8 +380,7 @@
         grads = dt[...]
         return dot(k, grads, TN).T, dot(grads, hq[h]), dot(pr[h], hg[h])
 
-    cot_relay()
-    cot_flow((1, 2, 3))
+    cot_flow((3,))
     for d in range(1, NY):
         x_copy(d, False).wait_recv()
     x_own.wait()

time: 95.7 us -> 94.8 us (level)
  no operation moved by 1% of the time
where the time goes in v7:
time: 94.8 us; the launch traced here: 94.7 us
  Pallas kernels  91.6 us (97%)
  local copies, waits for them, and re-layouts  1.84 us (2%)
  between operations  1.28 us (1%)
    pallas_call x1, Pallas kernels, on_device(): pl.pallas_call(kernel, out_shape=(jax.ShapeDtypeStruct((3, 2 * POS, WIDTH...  91.6 us

profile of v7, /device:TPU:1, one launch (start us, length us, event | category | flops | bytes accessed | tf_op | source)
XLA Modules:
  0.0 94.7 jit_solution(8712153926484605779)
XLA Ops:
  1.3 91.6 %layer.1 = (bf16[3,128,1280]{2,1,0:T(8,128)(2,1)S(1)}, f32[160,1280]{1,0:T(8,128)S(1)}) custom-call(s32[1]{0:T(128)S(6)} %copy.8.vc_ref, bf16[3,128,1280]{2,1,0:T(8,128)(2,1)} %qkv_hbm.1, bf16[128,1280]{1,0:T(8,128)(2,1)} %cot_hbm.1, bf16[1280,1280]{1,0:T(8,128)(2,1)} %w_ref.1), custom_call_target="tpu_custom_call" | custom-call | tf_op jit(solution)/shard_map/layer/pallas_call | solution.py:616
  92.8 0.9 %copy.9 = bf16[3,128,1280]{2,1,0:T(8,128)(2,1)} copy(bf16[3,128,1280]{2,1,0:T(8,128)(2,1)S(1)} %get-tuple-element.4) | data formatting | bytes 1966080
  93.8 0.9 copy.10
